TPU v7x, 32 devices: a whole 2x2x4 slice. The times are simulated.
32 devices in a mesh: blk: 2 (over x), wide: 16 (over z, y, core).
Axes of the slice: x: 2, y: 2, z: 4, core: 2. Of those that a mesh axis runs over, the one named last changes fastest.
Arguments:
- resid: bfloat16 [8192, 1024], P('wide', 'blk'), may hold values from -24 to 24
- samples: bfloat16 [8192, 1024], P('wide', 'blk'), may hold values from -6 to 6
- precision: float32 [64, 2, 32, 128, 128], P('wide', 'blk'), as said below
- active: int32 [64, 2, 32], P('wide', 'blk'), may hold values 0 or 1
Outputs:
- updated: float32 [64, 2, 32, 128, 128], P('wide', 'blk')
Inputs may be any that keep to these rules, and one draw needn't show every extreme that they name: `precision`: entries on the diagonal of W lie between 1 and 2.
All inputs are finite; a program needn't handle non-finite values. No bound on the sum of `active` on one device may be relied on, other than what follows from the above.
Results may differ from a plain program's by a relative error of at most 0.0003.
Values may be sent and summed in bfloat16 or wider, within the bound.
A program may use at most 192 MiB of HBM per device.

v0:
```python
import functools

import jax
import jax.numpy as jnp
from jax import lax
from jax.experimental import pallas as pl
from jax.experimental.pallas import tpu as pltpu
from jax.sharding import PartitionSpec as P

STEP = 1.0
LASSO = 0.1
RIDGE = 0.5


def local(resid, samples, precision, active):
    groups = lax.axis_size("blk")
    column_group = lax.axis_index("blk")
    panel_index = lax.axis_index("wide")
    row_tiles = precision.shape[0]
    per_class = precision.shape[2]
    tile_size = precision.shape[3]
    tiles = per_class * groups
    local_samples = resid.shape[1]
    total_samples = local_samples * groups
    own_rows = panel_index * row_tiles + jnp.arange(row_tiles, dtype=jnp.int32)
    first_column = (column_group - own_rows) % groups
    own_resid = resid.reshape(row_tiles, tile_size, local_samples)
    own_data = samples.reshape(row_tiles, tile_size, local_samples)
    all_resid, all_data = (
        lax.all_gather(resid, "wide", axis=0, tiled=True),
        lax.all_gather(samples, "wide", axis=0, tiled=True),
    )
    resid_tiles = all_resid.reshape(tiles, tile_size, local_samples)
    data_tiles = all_data.reshape(tiles, tile_size, local_samples)
    positions = jnp.arange(per_class * lax.axis_size("blk"), dtype=jnp.int32)
    classes = positions // per_class
    within = positions % per_class
    column_ids = (classes[:, None] - own_rows[None, :]) % groups + groups * within[:, None]
    forward = jnp.einsum(
        "kis,pkjs->pkij", own_resid, data_tiles[column_ids], preferred_element_type=jnp.float32
    )
    backward = jnp.einsum(
        "kis,pkjs->pkij", own_data, resid_tiles[column_ids], preferred_element_type=jnp.float32
    )
    summed = (
        lax.psum_scatter(0.5 * (forward + backward), "blk", scatter_dimension=0, tiled=True)
        / total_samples
    )
    precision_tiles = precision[:, 0]
    active_flags = active[:, 0].astype(jnp.float32)
    gradient_part = summed.transpose(1, 0, 2, 3)
    column_ids = first_column[:, None] + groups * jnp.arange(per_class, dtype=jnp.int32)[None, :]
    same_tile = column_ids == own_rows[:, None]
    identity = jnp.eye(tile_size, dtype=bool)
    on_diag = same_tile[:, :, None, None] & identity
    inverse = jnp.where(on_diag, 1.0 / jnp.where(on_diag, precision_tiles, 1.0), 0.0)
    stepped = precision_tiles - STEP * (gradient_part + RIDGE * precision_tiles - inverse)
    shrunk = jnp.sign(stepped) * jnp.maximum(jnp.abs(stepped) - STEP * LASSO, 0.0)
    updated = jnp.where(on_diag, stepped, shrunk) * active_flags[:, :, None, None]
    return updated[:, None]


MESH = pl.DeviceIdType.MESH


def pick(table, i):
    value = jnp.int32(table[0])
    for n in range(1, len(table)):
        value = jnp.where(i == n, jnp.int32(table[n]), value)
    return value


def kernel(
    depth, scale, resid, samples, weights, flags, held,
    own, cols, mate, stage, landed, recv, own_recv, res_recv, mate_recv, send, own_send, res_send,
    mate_send, fill,
):
    b = lax.axis_index("blk")
    w = lax.axis_index("wide")
    nb = 1 - b
    z, y, c = w // 4, (w // 2) % 2, w % 2
    per = own.shape[2]
    tile = own.shape[4]
    panels = cols.shape[1]
    up, down = (z + 1 < depth), (z > 0)
    last = depth - 1
    inner = jnp.where(up, 1, 0) * jnp.where(down, 1, 0)
    far = jnp.where(2 * z < depth, 1, 0)
    far_z = far * last

    def at(zz, yy, cc):
        return (zz * 2 + yy) * 2 + cc

    orders = [
        sorted((o for o in range(depth) if o != i), key=lambda o: (abs(o - i), o))
        for i in range(depth)
    ]

    def order(k):
        value = z
        for n in range(1, depth):
            value = jnp.where(k == n, pick([orders[i][n - 1] for i in range(depth)], z), value)
        return value

    loads = []
    for a, src in enumerate((resid, samples)):
        for p in range(2):
            loads.append(
                pltpu.make_async_copy(src.at[:, p], own.at[b, p, :, a], fill.at[2 * a + p])
            )
    for load in loads:
        load.start()
    load_weights = pltpu.make_async_copy(weights, held, fill.at[4])

    barrier = pltpu.get_barrier_semaphore()

    def greet(**device):
        pl.semaphore_signal(barrier, inc=1, device_id=device, device_id_type=MESH)

    greet(blk=nb)
    greet(wide=at(z, 1 - y, c))
    greet(wide=at(z, y, 1 - c))

    @pl.when(up)
    def _():
        greet(wide=at(z + 1, y, c))

    @pl.when(down)
    def _():
        greet(wide=at(z - 1, y, c))

    pl.semaphore_wait(barrier, 3 + jnp.where(up, 1, 0) + jnp.where(down, 1, 0))

    def push(h, t, src, panel, k, lane, target):
        return pltpu.make_async_remote_copy(
            src_ref=src, dst_ref=cols.at[h, panel, t], send_sem=send.at[h, t, k, lane],
            recv_sem=recv.at[h, panel, t], device_id={"wide": target}, device_id_type=MESH,
        )

    def arrive(h, t, panel):
        push(h, t, cols.at[h, panel, t], panel, 0, 0, at(z, 1 - y, c)).wait_recv()

    def own_pushes(h, t):
        src = own.at[h, b, t]
        return (
            (up, push(h, t, src, w, 0, 0, at(z + 1, y, c))),
            (down, push(h, t, src, w, 0, 1, at(z - 1, y, c))),
            (None, push(h, t, src, w, 0, 2, at(z, 1 - y, c))),
            (None, push(h, t, src, w, 0, 3, at(z, y, 1 - c))),
        )

    def z_pushes(h, t, k):
        zk = order(k)
        panel = at(zk, y, c)
        src = cols.at[h, panel, t]
        onward = jnp.where(zk < z, z + 1, z - 1)
        exists = jnp.logical_and(onward >= 0, onward < depth)
        return (
            (exists, push(h, t, src, panel, k, 0, at(onward, y, c))),
            (None, push(h, t, src, panel, k, 2, at(z, 1 - y, c))),
            (None, push(h, t, src, panel, k, 3, at(z, y, 1 - c))),
        )

    def y_push(h, t, k):
        panel = at(order(k), 1 - y, c)
        return ((None, push(h, t, cols.at[h, panel, t], panel, k, 4, at(z, y, 1 - c))),)

    def mate_push(h, src, slot, lane, target):
        return pltpu.make_async_remote_copy(
            src_ref=src, dst_ref=mate.at[h, slot], send_sem=mate_send.at[h, lane],
            recv_sem=mate_recv.at[h, slot], device_id={"wide": target}, device_id_type=MESH,
        )

    def beside_push(h):
        return ((None, mate_push(h, own.at[h, nb], 0, 0, at(z, y, 1 - c))),)

    def end_push(h):
        slot = jnp.where(z == 0, 1, 2)
        inward = jnp.where(z == 0, z + 1, z - 1)
        return ((inner == 0, mate_push(h, own.at[h, nb], slot, 1, at(inward, y, c))),)

    def relay_push(h, end, lane):
        onward = jnp.where(end == 0, z + 1, z - 1)
        return ((inner == 1, mate_push(h, mate.at[h, 1 + end], 1 + end, lane, at(onward, y, c))),)

    def far_push(h):
        return ((None, mate_push(h, mate.at[h, 1 + far], 3, 4, at(z, y, 1 - c))),)

    def mate_arrive(h, slot):
        mate_push(h, mate.at[h, slot], slot, 0, at(z, y, 1 - c)).wait_recv()

    def start(pushes):
        for when, copy in pushes:
            if when is None:
                copy.start()
            else:
                pl.when(when)(copy.start)

    def drain(pushes):
        for when, copy in pushes:
            if when is None:
                copy.wait_send()
            else:
                pl.when(when)(copy.wait_send)

    def forward_z(k):
        for t in range(per):
            for h in (b, nb):
                arrive(h, t, at(order(k), y, c))
                start(z_pushes(h, t, k))

    def relay_near(h):
        @pl.when(inner == 1)
        def _():
            mate_arrive(h, 2 - far)
            start(relay_push(h, 1 - far, 2))

    def relay_far(h):
        mate_arrive(h, 1 + far)
        start(relay_push(h, far, 3))
        start(far_push(h))

    def swap(h, i, t):
        p = (nb, b)[i] if h is b else (b, nb)[i]
        return pltpu.make_async_remote_copy(
            src_ref=own.at[h, p, t], dst_ref=own.at[h, p, t], send_sem=own_send.at[i, t],
            recv_sem=own_recv.at[i, t], device_id={"blk": nb}, device_id_type=MESH,
        )

    def hand(panel, u):
        return pltpu.make_async_remote_copy(
            src_ref=stage.at[panel, u], dst_ref=landed.at[panel, u],
            send_sem=res_send.at[panel, u], recv_sem=res_recv.at[panel, u],
            device_id={"blk": nb}, device_id_type=MESH,
        )

    def gram(p, side):
        total = None
        for h in range(2):
            for a in range(2):
                left = own[h, p, :, a].reshape(per * tile, -1)
                right = side(h, 1 - a).reshape(-1, own.shape[5])
                part = lax.dot_general(
                    left, right, (((1,), (1,)), ((), ())), preferred_element_type=jnp.float32
                )
                total = part if total is None else total + part
        return total * scale

    def finish(p, panel, u, part, diagonal):
        for t in range(per):
            slot = panel * per + u
            weight = held[t, p, slot]
            half = part(t) + RIDGE * weight
            if diagonal and t == u:
                rows = lax.broadcasted_iota(jnp.int32, (tile, tile), 0)
                columns = lax.broadcasted_iota(jnp.int32, (tile, tile), 1)
                on_diag = rows == columns + b * (2 * tile)
                inverse = jnp.where(on_diag, 1.0 / jnp.where(on_diag, weight, 1.0), 0.0)
                stepped = weight - STEP * (half - inverse)
            else:
                stepped = weight - STEP * half
            bound = STEP * LASSO
            updated = stepped - jnp.clip(stepped, -bound, bound)
            if diagonal and t == u:
                updated = jnp.where(on_diag, stepped, updated)
            flag = flags[2 * t + p, slot].astype(jnp.float32)
            held[t, p, slot] = updated * flag

    def cut(total, u=0):
        return lambda t: total[t * tile:(t + 1) * tile, u * tile:(u + 1) * tile]

    def finish_all(p, panel, total, diagonal):
        for u in range(per):
            finish(p, panel, u, cut(total, u), diagonal)

    for load in loads:
        load.wait()
    for i in range(2):
        for t in range(per):
            swap(b, i, t).start()
    for t in range(per):
        start(own_pushes(b, t))
    load_weights.start()
    for t in range(per):
        swap(nb, 0, t).wait_recv()
        start(own_pushes(nb, t))
    start(end_push(b))
    start(beside_push(b))
    for h in (b, nb):
        for t in range(per):
            arrive(h, t, at(order(1), y, c))
            start(z_pushes(h, t, 1))

            @pl.when(inner == 1)
            def _():
                arrive(h, t, at(order(2), y, c))
                start(z_pushes(h, t, 2)[:1])
    for t in range(per):
        swap(nb, 1, t).wait_recv()
    start(end_push(nb))
    load_weights.wait()

    def place(n):
        s = n + 2 + jnp.where(n < 4 * depth - 6, 0, 2)
        k, i = s // 4, s % 4
        yy = jnp.where(i < 2, y, 1 - y)
        cc = jnp.where(i % 2 == 0, c, 1 - c)
        return k, i, at(order(k), yy, cc)

    steps = 4 * depth - 4
    middle = steps - 4

    def receive(n, carry):
        panel = place(n)[2]
        for u in range(per):
            hand(panel, u).wait_recv()
            finish(1, panel, u, lambda t: landed[panel, u, t], False)
        return carry

    def keep(panel):
        finish_all(0, panel, gram(0, lambda h, a: cols[h, panel, :, a]), False)

    def nearby():
        for p in range(2):
            parity = b if p == 0 else nb
            finish_all(p, w, gram(p, lambda h, a: own[h, parity, :, a]), True)
        panel = at(z, y, 1 - c)
        for h in (b, nb):
            for t in range(per):
                arrive(h, t, panel)
            mate_arrive(h, 0)
        keep(panel)
        finish_all(1, panel, gram(1, lambda h, a: mate[h, 0, :, a]), False)

    def compute(n, carry):
        k, i, panel = place(n)
        ahead = k + 1 + inner

        @pl.when(jnp.logical_and(i == 2, k == 1))
        def _():
            nearby()

        @pl.when(jnp.logical_and(n == 0, inner == 1))
        def _():
            for t in range(per):
                for h in (b, nb):
                    start(z_pushes(h, t, 2)[1:])

        @pl.when(jnp.logical_and(i == 2, jnp.logical_and(k > 0, ahead < depth)))
        def _():
            forward_z(ahead)

        @pl.when(jnp.logical_and(i == 2, k == 1))
        def _():
            relay_near(b)

        @pl.when(jnp.logical_and(i == 2, k == last - inner))
        def _():
            relay_far(b)

        @pl.when(jnp.logical_and(i == 2, k == last))
        def _():
            lax.fori_loop(0, middle, receive, 0)

        for u in range(per):
            @pl.when(i != 0)
            def _():
                for h in (b, nb):
                    arrive(h, u, panel)

            @pl.when(i == 2)
            def _():
                for h in (b, nb):
                    start(y_push(h, u, k))

            total = cut(gram(1, lambda h, a: cols[h, panel, u, a]))
            for t in range(per):
                stage[panel, u, t] = total(t)
            hand(panel, u).start()

        @pl.when(n == 0)
        def _():
            start(beside_push(nb))

        @pl.when(k < last)
        def _():
            keep(panel)

        @pl.when(jnp.logical_and(i == 3, k == 1))
        def _():
            relay_near(nb)

        @pl.when(jnp.logical_and(i == 3, jnp.logical_and(k == 2, inner == 1)))
        def _():
            relay_far(nb)

        return carry

    lax.fori_loop(0, steps, compute, 0)

    def keep_late(n, carry):
        keep(place(n)[2])
        return carry

    lax.fori_loop(steps - 2, steps, keep_late, 0)

    @pl.when(inner == 0)
    def _():
        relay_far(nb)

    def distant(n, carry):
        cc = jnp.where(n == 0, c, 1 - c)
        slot = jnp.where(n == 0, 1 + far, 3)
        panel = at(far_z, y, cc)

        @pl.when(n == 1)
        def _():
            for h in (b, nb):
                for t in range(per):
                    arrive(h, t, panel)
                mate_arrive(h, 3)

        keep(panel)
        finish_all(1, panel, gram(1, lambda h, a: mate[h, slot, :, a]), False)
        return carry

    lax.fori_loop(0, 2, distant, 0)
    lax.fori_loop(middle, steps, receive, 0)

    for i in range(2):
        for t in range(per):
            swap(b, i, t).wait_send()
    for h in (b, nb):
        for t in range(per):
            drain(own_pushes(h, t))
        drain(beside_push(h))
        drain(end_push(h))
        drain(relay_push(h, 1 - far, 2))
        drain(relay_push(h, far, 3))
        drain(far_push(h))

    def drain_group(k, carry):
        for h in (b, nb):
            for t in range(per):
                drain(y_push(h, t, k))

                @pl.when(k > 0)
                def _():
                    drain(z_pushes(h, t, k))
        return carry

    lax.fori_loop(0, depth, drain_group, 0)

    def drain_panel(n, carry):
        for u in range(per):
            hand(place(n)[2], u).wait_send()
        return carry

    lax.fori_loop(0, steps, drain_panel, 0)


def ring(resid, samples, precision, active):
    panels = lax.axis_size("wide")
    row_tiles, _, per_class, tile, _ = precision.shape
    per = row_tiles // 2
    half = resid.shape[1]
    depth = panels // 4
    scale = 0.5 / (2 * half)
    any_spec = pl.BlockSpec(memory_space=pl.ANY)
    bf16, f32 = resid.dtype, jnp.float32
    dma = pltpu.SemaphoreType.DMA
    updated = pl.pallas_call(
        functools.partial(kernel, depth, scale),
        out_shape=pltpu.VMEM((per, 2, per_class, tile, tile), f32),
        in_specs=[any_spec, any_spec, any_spec, pl.BlockSpec(memory_space=pltpu.SMEM)],
        out_specs=pl.BlockSpec(memory_space=pltpu.VMEM),
        scratch_shapes=[
            pltpu.VMEM((2, 2, per, 2, tile, half), bf16),
            pltpu.VMEM((2, panels, per, 2, tile, half), bf16),
            pltpu.VMEM((2, 4, per, 2, tile, half), bf16),
            pltpu.VMEM((panels, per, per, tile, tile), f32),
            pltpu.VMEM((panels, per, per, tile, tile), f32),
            dma((2, panels, per)),
            dma((2, per)),
            dma((panels, per)),
            dma((2, 4)),
            dma((2, per, depth, 5)),
            dma((2, per)),
            dma((panels, per)),
            dma((2, 5)),
            dma((5,)),
        ],
        compiler_params=pltpu.CompilerParams(
            collective_id=0, has_side_effects=True, vmem_limit_bytes=52 * 1024 * 1024
        ),
    )(
        resid.reshape(per, 2, tile, half),
        samples.reshape(per, 2, tile, half),
        precision.reshape(per, 2, per_class, tile, tile),
        active[:, 0],
    )
    return updated.reshape(precision.shape)


def body(resid, samples, precision, active):
    panels = lax.axis_size("wide")
    row_tiles, _, per_class, tile, _ = precision.shape
    words = 8 * per_class * row_tiles * tile * tile + 4 * panels * row_tiles * tile * resid.shape[1]
    if lax.axis_size("blk") == 2 and panels // 4 == 4 and row_tiles % 2 == 0 and words < 52 * 1024 * 1024:
        return ring(resid, samples, precision, active)
    return local(resid, samples, precision, active)


def solution(mesh):
    in_specs = (
        P("wide", "blk"),
        P("wide", "blk"),
        P("wide", "blk", None, None, None),
        P("wide", "blk", None),
    )
    out_specs = P("wide", "blk", None, None, None)
    return jax.shard_map(body, mesh=mesh, in_specs=in_specs, out_specs=out_specs, check_vma=False)
```

profile of v0, /device:TPU:0, one launch (start us, length us, event | category | flops | bytes accessed | tf_op | source)
XLA Modules:
  0.0 112.1 jit_solution(17689262707071848275)
XLA Ops:
  0.0 108.7 %shard_map.46 = f32[2,2,32,128,128]{4,3,2,1,0:T(8,128)S(1)} custom-call(bf16[2,2,128,512]{3,2,1,0:T(8,128)(2,1)} %bitcast.9, bf16[2,2,128,512]{3,2,1,0:T(8,128)(2,1)} %bitcast.10, f32[2,2,32,128,128]{4,3,2,1,0:T(8,128)} %bitcast.8, s32[4,32]{1,0:T(4,128)} %bitcast.11), custom_call_target="tpu_custom_call" | custom-call | tf_op jit(solution)/shard_map/pallas_call | solution.py:472
  108.7 3.4 %copy.7 = f32[4,1,32,128,128]{4,3,2,1,0:T(8,128)} copy(f32[4,1,32,128,128]{4,3,2,1,0:T(8,128)S(1)} %bitcast.7) | data formatting | bytes 16777216
where the time goes:
time: 112 us
  Pallas kernels  109 us (97%)
  local copies, waits for them, and re-layouts  3.4 us (3%)
    pallas_call x1, Pallas kernels, ring(): pl.pallas_call(functools.partial(kernel, depth, scale), out_shape=pltpu.V...  109 us
    unnamed x1, local copies, waits for them, and re-layouts  3.4 us

commit v1 on v0

v1 whole, which is shorter than its diff:
```python
import functools

import jax
import jax.numpy as jnp
from jax import lax
from jax.experimental import pallas as pl
from jax.experimental.pallas import tpu as pltpu
from jax.sharding import PartitionSpec as P

STEP = 1.0
LASSO = 0.1
RIDGE = 0.5


def local(resid, samples, precision, active):
    groups = lax.axis_size("blk")
    column_group = lax.axis_index("blk")
    panel_index = lax.axis_index("wide")
    row_tiles = precision.shape[0]
    per_class = precision.shape[2]
    tile_size = precision.shape[3]
    tiles = per_class * groups
    local_samples = resid.shape[1]
    total_samples = local_samples * groups
    own_rows = panel_index * row_tiles + jnp.arange(row_tiles, dtype=jnp.int32)
    first_column = (column_group - own_rows) % groups
    own_resid = resid.reshape(row_tiles, tile_size, local_samples)
    own_data = samples.reshape(row_tiles, tile_size, local_samples)
    all_resid, all_data = (
        lax.all_gather(resid, "wide", axis=0, tiled=True),
        lax.all_gather(samples, "wide", axis=0, tiled=True),
    )
    resid_tiles = all_resid.reshape(tiles, tile_size, local_samples)
    data_tiles = all_data.reshape(tiles, tile_size, local_samples)
    positions = jnp.arange(per_class * lax.axis_size("blk"), dtype=jnp.int32)
    classes = positions // per_class
    within = positions % per_class
    column_ids = (classes[:, None] - own_rows[None, :]) % groups + groups * within[:, None]
    forward = jnp.einsum(
        "kis,pkjs->pkij", own_resid, data_tiles[column_ids], preferred_element_type=jnp.float32
    )
    backward = jnp.einsum(
        "kis,pkjs->pkij", own_data, resid_tiles[column_ids], preferred_element_type=jnp.float32
    )
    summed = (
        lax.psum_scatter(0.5 * (forward + backward), "blk", scatter_dimension=0, tiled=True)
        / total_samples
    )
    precision_tiles = precision[:, 0]
    active_flags = active[:, 0].astype(jnp.float32)
    gradient_part = summed.transpose(1, 0, 2, 3)
    column_ids = first_column[:, None] + groups * jnp.arange(per_class, dtype=jnp.int32)[None, :]
    same_tile = column_ids == own_rows[:, None]
    identity = jnp.eye(tile_size, dtype=bool)
    on_diag = same_tile[:, :, None, None] & identity
    inverse = jnp.where(on_diag, 1.0 / jnp.where(on_diag, precision_tiles, 1.0), 0.0)
    stepped = precision_tiles - STEP * (gradient_part + RIDGE * precision_tiles - inverse)
    shrunk = jnp.sign(stepped) * jnp.maximum(jnp.abs(stepped) - STEP * LASSO, 0.0)
    updated = jnp.where(on_diag, stepped, shrunk) * active_flags[:, :, None, None]
    return updated[:, None]


MESH = pl.DeviceIdType.MESH

END = (
    (1, 0, 0, 0, 1, 1), (0, 1, 0, 1, 0, 1), (1, 0, 1, 0, 1, 0), (0, 1, 1, 1, 0, 0),
    (2, 0, 0, 0, 1, 1), (1, 1, 0, 0, 0, 1), (2, 0, 1, 0, 1, 1), (1, 1, 1, 0, 0, 1),
    (3, 0, 0, 0, 0, 1), (2, 1, 0, 0, 0, 1), (3, 0, 1, 0, 1, 1), (2, 1, 1, 0, 0, 1),
    (3, 1, 0, 0, 0, 1), (3, 1, 1, 0, 0, 1),
)
INNER = (
    (2, 0, 0, 2, 1, 1), (0, 0, 0, 1, 0, 1), (1, 1, 0, 0, 0, 1), (2, 0, 1, 2, 1, 1),
    (0, 0, 1, 1, 0, 0), (1, 1, 1, 0, 0, 0), (3, 0, 0, 2, 0, 1), (0, 1, 0, 1, 0, 1),
    (2, 1, 0, 0, 0, 1), (3, 0, 1, 2, 0, 1), (0, 1, 1, 1, 0, 1), (2, 1, 1, 0, 0, 1),
    (3, 1, 0, 2, 0, 1), (3, 1, 1, 0, 0, 1),
)
STEPS = len(END)
EARLY = 4
LAG = 6
OWN = STEPS


def packed(row):
    place, across, u, along, over, handed = row
    return place + 4 * across + 8 * u + 16 * along + 64 * over + 128 * handed


def kernel(
    depth, scale, resid, samples, weights, flags, held,
    own, cols, beside, near, stage, landed, recv, own_recv, res_recv, beside_recv, near_recv, send,
    own_send, res_send, beside_send, near_send, fill,
):
    b = lax.axis_index("blk")
    w = lax.axis_index("wide")
    nb = 1 - b
    z, y, c = w // 4, (w // 2) % 2, w % 2
    per = own.shape[2]
    tile = own.shape[4]
    last = depth - 1
    half = z // 2
    inner = jnp.where(z == 0, 0, jnp.where(z == last, 0, 1))
    inward = z + 1 - 2 * half
    outward = jnp.where(inner == 1, z - 1 + 2 * half, inward)

    def at(zz, yy, cc):
        return (zz * 2 + yy) * 2 + cc

    in_target, out_target = at(inward, y, c), at(outward, y, c)
    y_target, c_target = at(z, 1 - y, c), at(z, y, 1 - c)
    pair_target = jnp.where(inner == 1, out_target, in_target)

    def decode(n):
        end, mid = jnp.int32(packed(END[0])), jnp.int32(packed(INNER[0]))
        for k in range(1, STEPS):
            end = jnp.where(n == k, jnp.int32(packed(END[k])), end)
            mid = jnp.where(n == k, jnp.int32(packed(INNER[k])), mid)
        code = jnp.where(inner == 1, mid, end)
        place = code % 4
        zz = jnp.where(half == 0, place, last - place)
        yy = jnp.where((code // 4) % 2 == 1, 1 - y, y)
        u = (code // 8) % 2
        along = (code // 16) % 4
        over = (code // 64) % 2
        handed = code // 128
        return at(zz, yy, c), at(zz, yy, 1 - c), u, along, over, handed

    loads = []
    for a, src in enumerate((resid, samples)):
        for p in range(2):
            loads.append(
                pltpu.make_async_copy(src.at[:, p], own.at[b, p, :, a], fill.at[2 * a + p])
            )
    for load in loads:
        load.start()
    load_weights = pltpu.make_async_copy(weights, held, fill.at[4])

    barrier = pltpu.get_barrier_semaphore()

    def greet(**device):
        pl.semaphore_signal(barrier, inc=1, device_id=device, device_id_type=MESH)

    greet(blk=nb)
    greet(wide=y_target)
    greet(wide=c_target)
    greet(wide=in_target)

    @pl.when(inner == 1)
    def _():
        greet(wide=out_target)

    pl.semaphore_wait(barrier, 4 + inner)

    def push(h, u, src, panel, k, lane, target):
        return pltpu.make_async_remote_copy(
            src_ref=src, dst_ref=cols.at[h, panel, u], send_sem=send.at[h, u, k, lane],
            recv_sem=recv.at[h, panel, u], device_id={"wide": target}, device_id_type=MESH,
        )

    def arrive(h, u, panel):
        push(h, u, cols.at[h, panel, u], panel, 0, 0, y_target).wait_recv()

    def own_pushes(h, u):
        src = own.at[h, b, u]
        return (
            (None, push(h, u, src, w, OWN, 2, y_target)),
            (None, push(h, u, src, w, OWN, 0, in_target)),
            (inner == 1, push(h, u, src, w, OWN, 1, out_target)),
            (None, push(h, u, src, w, OWN, 3, c_target)),
        )

    def step_pushes(h, n, step):
        panel, _, u, along, over, _ = step
        src = cols.at[h, panel, u]
        target = jnp.where(along == 1, in_target, out_target)
        return (
            (along > 0, push(h, u, src, panel, n, 0, target)),
            (over == 1, push(h, u, src, panel, n, 2, y_target)),
            (None, push(h, u, src, panel, n, 3, c_target)),
        )

    def beside_push(h):
        return ((None, pltpu.make_async_remote_copy(
            src_ref=own.at[h, nb], dst_ref=beside.at[h], send_sem=beside_send.at[h],
            recv_sem=beside_recv.at[h], device_id={"wide": c_target}, device_id_type=MESH,
        )),)

    def near_push(h, j, src, target):
        return ((None, pltpu.make_async_remote_copy(
            src_ref=src, dst_ref=near.at[h, j], send_sem=near_send.at[h, j],
            recv_sem=near_recv.at[h, j], device_id={"wide": target}, device_id_type=MESH,
        )),)

    def near_own(h, j):
        return near_push(h, j, own.at[h, nb, per - 1], y_target if j == 0 else pair_target)

    def near_relay(h, j):
        return near_push(h, j + 1, near.at[h, j], c_target)

    def near_arrive(h, j):
        near_push(h, j, near.at[h, j], c_target)[0][1].wait_recv()

    def start(pushes):
        for when, copy in pushes:
            if when is None:
                copy.start()
            else:
                pl.when(when)(copy.start)

    def drain(pushes):
        for when, copy in pushes:
            if when is None:
                copy.wait_send()
            else:
                pl.when(when)(copy.wait_send)

    def swap(h, i, t):
        p = (nb, b)[i] if h is b else (b, nb)[i]
        return pltpu.make_async_remote_copy(
            src_ref=own.at[h, p, t], dst_ref=own.at[h, p, t], send_sem=own_send.at[i, t],
            recv_sem=own_recv.at[i, t], device_id={"blk": nb}, device_id_type=MESH,
        )

    def hand(panel, u):
        return pltpu.make_async_remote_copy(
            src_ref=stage.at[panel, u], dst_ref=landed.at[panel, u],
            send_sem=res_send.at[panel, u], recv_sem=res_recv.at[panel, u],
            device_id={"blk": nb}, device_id_type=MESH,
        )

    def gram(p, side):
        total = None
        for h in range(2):
            for a in range(2):
                left = own[h, p, :, a].reshape(per * tile, -1)
                right = side(h, 1 - a).reshape(-1, own.shape[5])
                part = lax.dot_general(
                    left, right, (((1,), (1,)), ((), ())), preferred_element_type=jnp.float32
                )
                total = part if total is None else total + part
        return total * scale

    def finish(p, panel, u, part, diagonal=False):
        for t in range(per):
            slot = panel * per + u
            weight = held[t, p, slot]
            half = part(t) + RIDGE * weight
            if diagonal and t == u:
                rows = lax.broadcasted_iota(jnp.int32, (tile, tile), 0)
                columns = lax.broadcasted_iota(jnp.int32, (tile, tile), 1)
                on_diag = rows == columns + b * (2 * tile)
                inverse = jnp.where(on_diag, 1.0 / jnp.where(on_diag, weight, 1.0), 0.0)
                stepped = weight - STEP * (half - inverse)
            else:
                stepped = weight - STEP * half
            bound = STEP * LASSO
            updated = stepped - jnp.clip(stepped, -bound, bound)
            if diagonal and t == u:
                updated = jnp.where(on_diag, stepped, updated)
            flag = flags[2 * t + p, slot].astype(jnp.float32)
            held[t, p, slot] = updated * flag

    def cut(total, u=0):
        return lambda t: total[t * tile:(t + 1) * tile, u * tile:(u + 1) * tile]

    def finish_all(p, panel, total, diagonal=False):
        for u in range(per):
            finish(p, panel, u, cut(total, u), diagonal)

    def keep(panel):
        finish_all(0, panel, gram(0, lambda h, a: cols[h, panel, :, a]))

    def forward(n):
        step = decode(n)
        for h in (b, nb):
            arrive(h, step[2], step[0])
            start(step_pushes(h, n, step))

    for load in loads:
        load.wait()
    for i in range(2):
        for t in range(per):
            swap(b, i, t).start()
    for t in range(per):
        start(own_pushes(b, t))
    load_weights.start()
    start(beside_push(b))
    for t in range(per):
        swap(nb, 0, t).wait_recv()
        start(own_pushes(nb, t))

    def early(n, carry):
        forward(n)
        return carry

    lax.fori_loop(0, EARLY, early, 0)
    for t in range(per):
        swap(nb, 1, t).wait_recv()
    start(beside_push(nb))
    load_weights.wait()

    def receive(n):
        first, second, u, _, _, handed = decode(n)

        @pl.when(handed == 1)
        def _():
            for panel in (first, second):
                hand(panel, u).wait_recv()
                finish(1, panel, u, lambda t: landed[panel, u, t])

    def nearby():
        for p in range(2):
            parity = b if p == 0 else nb
            finish_all(p, w, gram(p, lambda h, a: own[h, parity, :, a]), True)
        for h in (b, nb):
            for u in range(per):
                arrive(h, u, c_target)
            beside_push(h)[0][1].wait_recv()
        keep(c_target)
        finish_all(1, c_target, gram(1, lambda h, a: beside[h, :, a]))

    def compute(n, carry):
        @pl.when(n >= EARLY)
        def _():
            forward(n)

        first, second, u, _, _, handed = decode(n)

        @pl.when(n == jnp.where(inner == 1, STEPS - 2, STEPS - 4))
        def _():
            for h in (b, nb):
                start(near_own(h, 0))
                start(near_own(h, 2))

        def both(i, carry):
            panel = jnp.where(i == 0, first, second)

            @pl.when(i == 1)
            def _():
                for h in (b, nb):
                    arrive(h, u, panel)

            @pl.when(handed == 1)
            def _():
                total = cut(gram(1, lambda h, a: cols[h, panel, u, a]))
                for t in range(per):
                    stage[panel, u, t] = total(t)
                hand(panel, u).start()

            @pl.when(u == per - 1)
            def _():
                keep(panel)

            return carry

        lax.fori_loop(0, 2, both, 0)

        @pl.when(n == EARLY - 1)
        def _():
            nearby()

        @pl.when(n >= LAG)
        def _():
            receive(n - LAG)

        return carry

    lax.fori_loop(0, STEPS, compute, 0)

    def settle(n, carry):
        receive(n)
        return carry

    lax.fori_loop(STEPS - LAG, STEPS - 2, settle, 0)

    for h in (b, nb):
        for j in (0, 2):
            near_arrive(h, j)
            start(near_relay(h, j))

    beyond = jnp.where(inner == 1, outward, inward)

    def adjacent(i, carry):
        j = jnp.where(i < 2, 2 * i, 2 * i - 3)
        zz = jnp.where(j < 2, z, beyond)
        yy = jnp.where(j < 2, 1 - y, y)
        cc = jnp.where(j % 2 == 0, c, 1 - c)

        @pl.when(i >= 2)
        def _():
            for h in (b, nb):
                near_arrive(h, j)

        total = gram(1, lambda h, a: near[h, j, a])
        finish(1, at(zz, yy, cc), per - 1, cut(total))
        return carry

    lax.fori_loop(0, 4, adjacent, 0)
    lax.fori_loop(STEPS - 2, STEPS, settle, 0)

    for i in range(2):
        for t in range(per):
            swap(b, i, t).wait_send()
    for h in (b, nb):
        for t in range(per):
            drain(own_pushes(h, t))
        drain(beside_push(h))
        for j in (0, 2):
            drain(near_own(h, j))
            drain(near_relay(h, j))

    def drain_step(n, carry):
        step = decode(n)
        for h in (b, nb):
            drain(step_pushes(h, n, step))

        @pl.when(step[5] == 1)
        def _():
            for panel in step[:2]:
                hand(panel, step[2]).wait_send()

        return carry

    lax.fori_loop(0, STEPS, drain_step, 0)


def ring(resid, samples, precision, active):
    panels = lax.axis_size("wide")
    row_tiles, _, per_class, tile, _ = precision.shape
    per = row_tiles // 2
    half = resid.shape[1]
    depth = panels // 4
    scale = 0.5 / (2 * half)
    any_spec = pl.BlockSpec(memory_space=pl.ANY)
    bf16, f32 = resid.dtype, jnp.float32
    dma = pltpu.SemaphoreType.DMA
    updated = pl.pallas_call(
        functools.partial(kernel, depth, scale),
        out_shape=pltpu.VMEM((per, 2, per_class, tile, tile), f32),
        in_specs=[any_spec, any_spec, any_spec, pl.BlockSpec(memory_space=pltpu.SMEM)],
        out_specs=pl.BlockSpec(memory_space=pltpu.VMEM),
        scratch_shapes=[
            pltpu.VMEM((2, 2, per, 2, tile, half), bf16),
            pltpu.VMEM((2, panels, per, 2, tile, half), bf16),
            pltpu.VMEM((2, per, 2, tile, half), bf16),
            pltpu.VMEM((2, 4, 2, tile, half), bf16),
            pltpu.VMEM((panels, per, per, tile, tile), f32),
            pltpu.VMEM((panels, per, per, tile, tile), f32),
            dma((2, panels, per)),
            dma((2, per)),
            dma((panels, per)),
            dma((2,)),
            dma((2, 4)),
            dma((2, per, STEPS + 1, 4)),
            dma((2, per)),
            dma((panels, per)),
            dma((2,)),
            dma((2, 4)),
            dma((5,)),
        ],
        compiler_params=pltpu.CompilerParams(
            collective_id=0, has_side_effects=True, vmem_limit_bytes=52 * 1024 * 1024
        ),
    )(
        resid.reshape(per, 2, tile, half),
        samples.reshape(per, 2, tile, half),
        precision.reshape(per, 2, per_class, tile, tile),
        active[:, 0],
    )
    return updated.reshape(precision.shape)


def body(resid, samples, precision, active):
    panels = lax.axis_size("wide")
    row_tiles, _, per_class, tile, _ = precision.shape
    words = 8 * per_class * row_tiles * tile * tile + 4 * panels * row_tiles * tile * resid.shape[1]
    if lax.axis_size("blk") == 2 and panels // 4 == 4 and row_tiles == 4 and words < 52 * 1024 * 1024:
        return ring(resid, samples, precision, active)
    return local(resid, samples, precision, active)


def solution(mesh):
    in_specs = (
        P("wide", "blk"),
        P("wide", "blk"),
        P("wide", "blk", None, None, None),
        P("wide", "blk", None),
    )
    out_specs = P("wide", "blk", None, None, None)
    return jax.shard_map(body, mesh=mesh, in_specs=in_specs, out_specs=out_specs, check_vma=False)
```

time: 112 us -> 107 us (0.955)
  Pallas kernels: 109 us -> 103 us
    pallas_call x1, Pallas kernels: 109 us -> 103 us  [ring(): pl.pallas_call(functools.partial(kernel, depth, scale), out_shape=pltpu.V...]
where the time goes in v1:
time: 107 us
  Pallas kernels  103 us (96%)
  local copies, waits for them, and re-layouts  3.4 us (3%)
    pallas_call x1, Pallas kernels, ring(): pl.pallas_call(functools.partial(kernel, depth, scale), out_shape=pltpu.V...  103 us
    unnamed x1, local copies, waits for them, and re-layouts  3.4 us

profile of v1, /device:TPU:0, one launch (start us, length us, event | category | flops | bytes accessed | tf_op | source)
XLA Modules:
  0.0 106.6 jit_solution(12309875709814954196)
XLA Ops:
  0.0 103.2 %shard_map.46 = f32[2,2,32,128,128]{4,3,2,1,0:T(8,128)S(1)} custom-call(bf16[2,2,128,512]{3,2,1,0:T(8,128)(2,1)} %bitcast.9, bf16[2,2,128,512]{3,2,1,0:T(8,128)(2,1)} %bitcast.10, f32[2,2,32,128,128]{4,3,2,1,0:T(8,128)} %bitcast.8, s32[4,32]{1,0:T(4,128)} %bitcast.11), custom_call_target="tpu_custom_call" | custom-call | tf_op jit(solution)/shard_map/pallas_call | solution.py:436
  103.2 3.4 %copy.7 = f32[4,1,32,128,128]{4,3,2,1,0:T(8,128)} copy(f32[4,1,32,128,128]{4,3,2,1,0:T(8,128)S(1)} %bitcast.7) | data formatting | bytes 16777216

commit v2 on v1

v2 whole, which is shorter than its diff:
```python
import functools

import jax
import jax.numpy as jnp
from jax import lax
from jax.experimental import pallas as pl
from jax.experimental.pallas import tpu as pltpu
from jax.sharding import PartitionSpec as P

STEP = 1.0
LASSO = 0.1
RIDGE = 0.5


def local(resid, samples, precision, active):
    groups = lax.axis_size("blk")
    column_group = lax.axis_index("blk")
    panel_index = lax.axis_index("wide")
    row_tiles = precision.shape[0]
    per_class = precision.shape[2]
    tile_size = precision.shape[3]
    tiles = per_class * groups
    local_samples = resid.shape[1]
    total_samples = local_samples * groups
    own_rows = panel_index * row_tiles + jnp.arange(row_tiles, dtype=jnp.int32)
    first_column = (column_group - own_rows) % groups
    own_resid = resid.reshape(row_tiles, tile_size, local_samples)
    own_data = samples.reshape(row_tiles, tile_size, local_samples)
    all_resid, all_data = (
        lax.all_gather(resid, "wide", axis=0, tiled=True),
        lax.all_gather(samples, "wide", axis=0, tiled=True),
    )
    resid_tiles = all_resid.reshape(tiles, tile_size, local_samples)
    data_tiles = all_data.reshape(tiles, tile_size, local_samples)
    positions = jnp.arange(per_class * lax.axis_size("blk"), dtype=jnp.int32)
    classes = positions // per_class
    within = positions % per_class
    column_ids = (classes[:, None] - own_rows[None, :]) % groups + groups * within[:, None]
    forward = jnp.einsum(
        "kis,pkjs->pkij", own_resid, data_tiles[column_ids], preferred_element_type=jnp.float32
    )
    backward = jnp.einsum(
        "kis,pkjs->pkij", own_data, resid_tiles[column_ids], preferred_element_type=jnp.float32
    )
    summed = (
        lax.psum_scatter(0.5 * (forward + backward), "blk", scatter_dimension=0, tiled=True)
        / total_samples
    )
    precision_tiles = precision[:, 0]
    active_flags = active[:, 0].astype(jnp.float32)
    gradient_part = summed.transpose(1, 0, 2, 3)
    column_ids = first_column[:, None] + groups * jnp.arange(per_class, dtype=jnp.int32)[None, :]
    same_tile = column_ids == own_rows[:, None]
    identity = jnp.eye(tile_size, dtype=bool)
    on_diag = same_tile[:, :, None, None] & identity
    inverse = jnp.where(on_diag, 1.0 / jnp.where(on_diag, precision_tiles, 1.0), 0.0)
    stepped = precision_tiles - STEP * (gradient_part + RIDGE * precision_tiles - inverse)
    shrunk = jnp.sign(stepped) * jnp.maximum(jnp.abs(stepped) - STEP * LASSO, 0.0)
    updated = jnp.where(on_diag, stepped, shrunk) * active_flags[:, :, None, None]
    return updated[:, None]


MESH = pl.DeviceIdType.MESH

END = (
    (1, 0, 0, 0, 1, 0, 2), (0, 1, 0, 1, 0, 1, 0), (0, 1, 1, 1, 0, 1, 1), (2, 0, 0, 0, 1, 1, 0),
    (2, 0, 1, 0, 1, 1, 1), (1, 1, 0, 0, 0, 1, 2), (3, 0, 0, 0, 1, 1, 0), (2, 1, 0, 0, 0, 1, 0),
    (3, 0, 1, 0, 1, 1, 1), (2, 1, 1, 0, 0, 1, 1), (3, 1, 0, 0, 0, 1, 0), (3, 1, 1, 0, 0, 1, 1),
)
INNER = (
    (2, 0, 0, 2, 1, 1, 0), (0, 0, 0, 1, 0, 1, 0), (1, 1, 0, 0, 0, 0, 0), (2, 0, 1, 2, 1, 0, 1),
    (0, 0, 1, 1, 0, 1, 1), (1, 1, 1, 0, 0, 0, 1), (3, 0, 0, 2, 0, 1, 0), (0, 1, 0, 1, 0, 1, 0),
    (2, 1, 0, 0, 0, 1, 0), (3, 0, 1, 2, 0, 1, 1), (0, 1, 1, 1, 0, 1, 1), (2, 1, 1, 0, 0, 1, 1),
    (3, 1, 0, 0, 0, 1, 0), (3, 1, 1, 0, 0, 1, 1),
)
STEPS = len(INNER)
EARLY = (3, 6)
LAG = 4
BATCH = 8
ALONG, OVER, CORE, HAND, SWAP, BESIDE, NEAR, PAIR, DIRECT, VIA, ONWARD = range(11)


def packed(row):
    place, across, u, along, over, handed, kept = row
    return place + 4 * across + 8 * u + 16 * along + 64 * over + 128 * handed + 256 * kept


def kernel(
    depth, scale, resid, samples, weights, flags, held,
    own, cols, beside, near, pair, stage, landed, out, got, passing, recv, beside_cols, own_recv,
    res_recv, beside_recv, near_recv, pair_recv, got_recv, passing_recv, sends, fill,
):
    b = lax.axis_index("blk")
    w = lax.axis_index("wide")
    nb = 1 - b
    z, y, c = w // 4, (w // 2) % 2, w % 2
    per = own.shape[2]
    tile = own.shape[4]
    last = depth - 1
    half = z // 2
    inner = jnp.where(z == 0, 0, jnp.where(z == last, 0, 1))
    inward = z + 1 - 2 * half
    outward = jnp.where(inner == 1, z - 1 + 2 * half, inward)

    def at(zz, yy, cc):
        return (zz * 2 + yy) * 2 + cc

    in_target, out_target = at(inward, y, c), at(outward, y, c)
    y_target, c_target = at(z, 1 - y, c), at(z, y, 1 - c)
    count = len(END) + (len(INNER) - len(END)) * inner
    ahead = EARLY[0] + (EARLY[1] - EARLY[0]) * inner

    def decode(n):
        end, mid = jnp.int32(packed(END[0])), jnp.int32(packed(INNER[0]))
        for k in range(1, STEPS):
            if k < len(END):
                end = jnp.where(n == k, jnp.int32(packed(END[k])), end)
            mid = jnp.where(n == k, jnp.int32(packed(INNER[k])), mid)
        code = jnp.where(inner == 1, mid, end)
        place = code % 4
        zz = jnp.where(half == 0, place, last - place)
        across = (code // 4) % 2
        yy = jnp.where(across == 1, 1 - y, y)
        u = (code // 8) % 2
        along = (code // 16) % 4
        over = (code // 64) % 2
        handed = (code // 128) % 2
        kept = code // 256
        served = jnp.where(place == 0, inner, 0)
        return at(zz, yy, c), at(zz, yy, 1 - c), u, along, over, handed, kept, across, served

    loads = []
    for a, src in enumerate((resid, samples)):
        for p in range(2):
            loads.append(
                pltpu.make_async_copy(src.at[:, p], own.at[b, p, :, a], fill.at[0])
            )
    for load in loads:
        load.start()
    load_weights = pltpu.make_async_copy(weights, held, fill.at[1])

    barrier = pltpu.get_barrier_semaphore()

    def greet(**device):
        pl.semaphore_signal(barrier, inc=1, device_id=device, device_id_type=MESH)

    greet(blk=nb)
    greet(wide=y_target)
    greet(wide=c_target)
    greet(wide=in_target)

    @pl.when(inner == 1)
    def _():
        greet(wide=out_target)

    greet(wide=at(outward, y, 1 - c))
    pl.semaphore_wait(barrier, 5 + inner)

    def whole(ref, sent_sem, took_sem):
        return pltpu.make_async_remote_copy(
            src_ref=ref, dst_ref=ref, send_sem=sent_sem, recv_sem=took_sem,
            device_id={"wide": y_target}, device_id_type=MESH,
        )

    def took(ref, sem):
        whole(ref, sends.at[0], sem).wait_recv()

    def sent(ref, k):
        whole(ref, sends.at[k], recv.at[0, 0, 0]).wait_send()

    def push(h, u, src, panel, lane, target):
        sem = beside_cols.at[panel // 2, u] if lane == CORE else recv.at[h, panel // 2, u]
        return pltpu.make_async_remote_copy(
            src_ref=src, dst_ref=cols.at[h, panel, u], send_sem=sends.at[lane],
            recv_sem=sem, device_id={"wide": target}, device_id_type=MESH,
        )

    def arrive(h, u, panel):
        took(cols.at[h, panel, u], recv.at[h, panel // 2, u])

    def arrive_beside(u, panel):
        took(cols.at[:, panel, u], beside_cols.at[panel // 2, u])

    def own_pushes(h, u):
        src = own.at[h, b, u]
        return (
            (None, push(h, u, src, w, OVER, y_target)),
            (None, push(h, u, src, w, ALONG, in_target)),
            (None, push(h, u, src, w, CORE, c_target)),
        ) + (((inner == 1, push(h, u, src, w, ALONG, out_target)),) if u == 0 else ())

    def step_pushes(h, step):
        panel, _, u, along, over = step[:5]
        src = cols.at[h, panel, u]
        target = jnp.where(along == 1, in_target, out_target)
        return (
            (along > 0, push(h, u, src, panel, ALONG, target)),
            (over == 1, push(h, u, src, panel, OVER, y_target)),
            (None, push(h, u, src, panel, CORE, c_target)),
        )

    def beside_push(h):
        return ((None, pltpu.make_async_remote_copy(
            src_ref=own.at[h, nb], dst_ref=beside.at[h], send_sem=sends.at[BESIDE],
            recv_sem=beside_recv.at[0], device_id={"wide": c_target}, device_id_type=MESH,
        )),)

    def near_push(h, d, u, src, target):
        return ((None, pltpu.make_async_remote_copy(
            src_ref=src, dst_ref=near.at[h, d, u], send_sem=sends.at[NEAR],
            recv_sem=near_recv.at[u if d == 0 else 2], device_id={"wide": target}, device_id_type=MESH,
        )),)

    def near_own(h, u):
        return near_push(h, 0, u, own.at[h, nb, u], y_target)

    def near_relay(h, u):
        return near_push(h, 1, u, near.at[h, 0, u], c_target)

    def near_arrive(u):
        took(near.at[:, 0, u], near_recv.at[u])

    def pair_push(h, d, src, target):
        return ((None, pltpu.make_async_remote_copy(
            src_ref=src, dst_ref=pair.at[h, d], send_sem=sends.at[PAIR],
            recv_sem=pair_recv.at[d], device_id={"wide": target}, device_id_type=MESH,
        )),)

    def pair_own(h):
        return pair_push(h, 0, own.at[h, nb, per - 1], in_target)

    def pair_relay(h):
        return pair_push(h, 1, pair.at[h, 0], c_target)

    def pair_arrive(d):
        took(pair.at[:, d], pair_recv.at[d])

    def outward_core(d):
        return at(outward, y, jnp.where(d == 0, c, 1 - c))

    def direct(d, p, u, t):
        return pltpu.make_async_remote_copy(
            src_ref=out.at[0, d, p, u, t], dst_ref=got.at[d, p, u, t],
            send_sem=sends.at[DIRECT], recv_sem=got_recv.at[0],
            device_id={"wide": outward_core(d)}, device_id_type=MESH,
        )

    def via(d, p, u):
        return pltpu.make_async_remote_copy(
            src_ref=out.at[1, d, p, u, per - 1], dst_ref=passing.at[d, p, u],
            send_sem=sends.at[VIA], recv_sem=passing_recv.at[p * (1 + u)],
            device_id={"wide": y_target}, device_id_type=MESH,
        )

    def onward(d, p, u):
        return pltpu.make_async_remote_copy(
            src_ref=passing.at[d, p, u], dst_ref=got.at[2 + d, p, u, per - 1],
            send_sem=sends.at[ONWARD], recv_sem=got_recv.at[1],
            device_id={"wide": outward_core(d)}, device_id_type=MESH,
        )

    def start(pushes):
        for when, copy in pushes:
            if when is None:
                copy.start()
            else:
                pl.when(when)(copy.start)

    def swap(h, i, t):
        p = (nb, b)[i] if h is b else (b, nb)[i]
        return pltpu.make_async_remote_copy(
            src_ref=own.at[h, p, t], dst_ref=own.at[h, p, t], send_sem=sends.at[SWAP],
            recv_sem=own_recv.at[t if i == 0 else 2], device_id={"blk": nb}, device_id_type=MESH,
        )

    def hand(panel, u):
        return pltpu.make_async_remote_copy(
            src_ref=stage.at[panel, u], dst_ref=landed.at[panel, u],
            send_sem=sends.at[HAND], recv_sem=res_recv.at[panel // 2, u],
            device_id={"blk": nb}, device_id_type=MESH,
        )

    def gram(p, side):
        total = None
        for h in range(2):
            for a in range(2):
                left = own[h, p, :, a].reshape(per * tile, -1)
                right = side(h, 1 - a).reshape(-1, own.shape[5])
                part = lax.dot_general(
                    left, right, (((1,), (1,)), ((), ())), preferred_element_type=jnp.float32
                )
                total = part if total is None else total + part
        return total * scale

    def finish(p, panel, u, part, diagonal=False):
        for t in range(per):
            slot = panel * per + u
            weight = held[t, p, slot]
            half = part(t) + RIDGE * weight
            if diagonal and t == u:
                rows = lax.broadcasted_iota(jnp.int32, (tile, tile), 0)
                columns = lax.broadcasted_iota(jnp.int32, (tile, tile), 1)
                on_diag = rows == columns + b * (2 * tile)
                inverse = jnp.where(on_diag, 1.0 / jnp.where(on_diag, weight, 1.0), 0.0)
                stepped = weight - STEP * (half - inverse)
            else:
                stepped = weight - STEP * half
            bound = STEP * LASSO
            updated = stepped - jnp.clip(stepped, -bound, bound)
            if diagonal and t == u:
                updated = jnp.where(on_diag, stepped, updated)
            flag = flags[2 * t + p, slot].astype(jnp.float32)
            held[t, p, slot] = updated * flag

    def cut(total, u=0):
        return lambda t: total[t * tile:(t + 1) * tile, u * tile:(u + 1) * tile]

    def finish_all(p, panel, total, diagonal=False):
        for u in range(per):
            finish(p, panel, u, cut(total, u), diagonal)

    def keep(panel):
        total = gram(0, lambda h, a: cols[h, panel, :, a])
        finish_all(0, panel, total)
        return total

    def emit(across, d, p, u, part):
        t = per - 1
        out[across, d, p, u, t] = part(t).T

        @pl.when(across == 1)
        def _():
            via(d, p, u).start()

        @pl.when(jnp.where(across == 0, nb, -1) == p)
        def _():
            for t in range(per - 1):
                out[0, d, p, u, t] = part(t).T

    def pass_on(h, step):
        arrive(h, step[2], step[0])
        start(step_pushes(h, step))

    def forward(n):
        step = decode(n)
        for h in (b, nb):
            pass_on(h, step)

    pltpu.make_async_copy(own.at[b], own.at[b], fill.at[0]).wait()
    for i in range(2):
        for t in range(per):
            swap(b, i, t).start()
    for t in range(per):
        start(own_pushes(b, t))
    load_weights.start()
    start(beside_push(b))
    for t in range(per):
        swap(nb, 0, t).wait_recv()
        start(own_pushes(nb, t))

    def early(n, carry):
        forward(n)
        return carry

    lax.fori_loop(0, ahead, early, 0)
    took(own.at[nb, nb], own_recv.at[2])
    start(beside_push(nb))
    load_weights.wait()

    def receive(n):
        step = decode(n)
        u, handed, across, served = step[2], step[5], step[7], step[8]

        @pl.when(handed == 1)
        def _():
            chip = step[0] // 2
            took(landed.at[pl.ds(2 * chip, 2), u], res_recv.at[chip, u])
            for d in range(2):
                panel = step[d]
                finish(1, panel, u, lambda t: landed[panel, u, t])

                @pl.when(served == 1)
                def _():
                    emit(across, d, 1, u, lambda t: landed[panel, u, t])

    def settle(n, carry):
        receive(n)
        return carry

    def nearby():
        for p in range(2):
            parity = b if p == 0 else nb
            finish_all(p, w, gram(p, lambda h, a: own[h, parity, :, a]), True)
        for u in range(per):
            arrive_beside(u, c_target)
        took(beside, beside_recv.at[0])
        keep(c_target)
        finish_all(1, c_target, gram(1, lambda h, a: beside[h, :, a]))

    def compute(n, carry):
        f = n + 2 * inner

        @pl.when(jnp.logical_and(f >= ahead, f < count))
        def _():
            forward(f)

        first, second, u, _, _, handed, kept, across, served = decode(n)

        def both(i, carry):
            panel = jnp.where(i == 0, first, second)

            @pl.when(i == 1)
            def _():
                arrive_beside(u, panel)

            @pl.when(handed == 1)
            def _():
                total = cut(gram(1, lambda h, a: cols[h, panel, u, a]))
                for t in range(per):
                    stage[panel, u, t] = total(t)
                hand(panel, u).start()

            @pl.when(kept == 1)
            def _():
                total = keep(panel)

                @pl.when(served == 1)
                def _():
                    for v in range(per):
                        emit(across, i, 0, v, cut(total, v))

            @pl.when(kept == 2)
            def _():
                finish(0, panel, u, cut(gram(0, lambda h, a: cols[h, panel, u, a])))

            return carry

        lax.fori_loop(0, 2, both, 0)

        @pl.when(n == ahead - 1)
        def _():
            nearby()

        @pl.when(n == BATCH)
        def _():
            lax.fori_loop(0, BATCH - LAG, settle, 0)

        @pl.when(n >= BATCH)
        def _():
            receive(n - LAG)

        @pl.when(inner == 1)
        def _():
            @pl.when(n == STEPS - 5)
            def _():
                for h in (b, nb):
                    start(near_own(h, 0))

            @pl.when(n == STEPS - 4)
            def _():
                for u in range(per):
                    for d in range(2):
                        for p in range(2):
                            direct(d, p, u, per - 1).start()
                        for t in range(per - 1):
                            direct(d, nb, u, t).start()

            @pl.when(n == STEPS - 2)
            def _():
                for h in (b, nb):
                    start(near_own(h, 1))
                    start(pair_own(h))
                relay(0)

            @pl.when(n == STEPS - 1)
            def _():
                relay(1)

        return carry

    def relay(k):
        p = min(k, 1)
        tiles = range(per) if k == 0 else (k - 1,)
        took(passing.at[:, p] if k == 0 else passing.at[:, p, k - 1], passing_recv.at[k])
        for u in tiles:
            for d in range(2):
                onward(d, p, u).start()

    lax.fori_loop(0, count, compute, 0)

    @pl.when(inner == 1)
    def _():
        receive(count - LAG)
        near_arrive(0)
        for h in (b, nb):
            start(near_relay(h, 0))
        relay(2)
        lax.fori_loop(count - LAG + 1, count - 2, settle, 0)
        near_arrive(1)
        for h in (b, nb):
            start(near_relay(h, 1))
        pair_arrive(0)
        for h in (b, nb):
            start(pair_relay(h))

        def adjacent(d, carry):
            cc = jnp.where(d == 0, c, 1 - c)

            @pl.when(d == 1)
            def _():
                took(near.at[:, 1], near_recv.at[2])
                pair_arrive(1)

            finish_all(1, at(z, 1 - y, cc), gram(1, lambda h, a: near[h, d, :, a]))
            finish(1, at(inward, y, cc), per - 1, cut(gram(1, lambda h, a: pair[h, d, a])))
            return carry

        lax.fori_loop(0, 2, adjacent, 0)

        sent(got.at[:3, :, :, 0], DIRECT)
        sent(passing, VIA)
        sent(passing, ONWARD)
        sent(near, NEAR)
        sent(pair, PAIR)
        sent(cols.at[0, :11], ALONG)
        sent(cols.at[0, :4], OVER)
        sent(cols.at[:, :8], CORE)

    @pl.when(inner == 0)
    def _():
        def accept(k, t, p):
            d = k % 2
            panel = at(inward, jnp.where(k < 2, y, 1 - y), jnp.where(d == 0, c, 1 - c))
            finish(jnp.where(p == 0, b, nb), panel, t, lambda u: got[k, p, u, t])

        def closer(k, carry):
            for t in range(per - 1):
                accept(k, t, nb)
            for p in range(2):
                accept(k, per - 1, p)
            return carry

        def farther(k, carry):
            accept(k % 2 + 2, per - 1, k // 2)
            return carry

        lax.fori_loop(count - LAG, count - 2, settle, 0)
        took(got.at[:3, :, :, 0], got_recv.at[0])
        lax.fori_loop(0, 2, closer, 0)
        took(got.at[2:, :, :, per - 1], got_recv.at[1])
        lax.fori_loop(0, 4, farther, 0)
        sent(cols.at[0, :4], ALONG)
        sent(cols.at[0, :7], OVER)
        sent(cols.at[:, :7], CORE)

    sent(own.at[b], SWAP)
    sent(beside, BESIDE)
    lax.fori_loop(count - 2, count, settle, 0)
    sent(stage.at[:11], HAND)


def ring(resid, samples, precision, active):
    panels = lax.axis_size("wide")
    row_tiles, _, per_class, tile, _ = precision.shape
    per = row_tiles // 2
    half = resid.shape[1]
    depth = panels // 4
    scale = 0.5 / (2 * half)
    any_spec = pl.BlockSpec(memory_space=pl.ANY)
    bf16, f32 = resid.dtype, jnp.float32
    dma = pltpu.SemaphoreType.DMA
    updated = pl.pallas_call(
        functools.partial(kernel, depth, scale),
        out_shape=pltpu.VMEM((per, 2, per_class, tile, tile), f32),
        in_specs=[any_spec, any_spec, any_spec, pl.BlockSpec(memory_space=pltpu.SMEM)],
        out_specs=pl.BlockSpec(memory_space=pltpu.VMEM),
        scratch_shapes=[
            pltpu.VMEM((2, 2, per, 2, tile, half), bf16),
            pltpu.VMEM((2, panels, per, 2, tile, half), bf16),
            pltpu.VMEM((2, per, 2, tile, half), bf16),
            pltpu.VMEM((2, 2, per, 2, tile, half), bf16),
            pltpu.VMEM((2, 2, 2, tile, half), bf16),
            pltpu.VMEM((panels, per, per, tile, tile), f32),
            pltpu.VMEM((panels, per, per, tile, tile), f32),
            pltpu.VMEM((2, 2, 2, per, per, tile, tile), f32),
            pltpu.VMEM((4, 2, per, per, tile, tile), f32),
            pltpu.VMEM((2, 2, per, tile, tile), f32),
            dma((2, panels // 2, per)),
            dma((panels // 2, per)),
            dma((3,)),
            dma((panels // 2, per)),
            dma((1,)),
            dma((3,)),
            dma((2,)),
            dma((2,)),
            dma((3,)),
            dma((11,)),
            dma((2,)),
        ],
        compiler_params=pltpu.CompilerParams(
            collective_id=0, has_side_effects=True, vmem_limit_bytes=52 * 1024 * 1024
        ),
    )(
        resid.reshape(per, 2, tile, half),
        samples.reshape(per, 2, tile, half),
        precision.reshape(per, 2, per_class, tile, tile),
        active[:, 0],
    )
    return updated.reshape(precision.shape)


def body(resid, samples, precision, active):
    panels = lax.axis_size("wide")
    row_tiles, _, per_class, tile, _ = precision.shape
    words = 8 * per_class * row_tiles * tile * tile + 4 * panels * row_tiles * tile * resid.shape[1]
    if lax.axis_size("blk") == 2 and panels // 4 == 4 and row_tiles == 4 and words < 52 * 1024 * 1024:
        return ring(resid, samples, precision, active)
    return local(resid, samples, precision, active)


def solution(mesh):
    in_specs = (
        P("wide", "blk"),
        P("wide", "blk"),
        P("wide", "blk", None, None, None),
        P("wide", "blk", None),
    )
    out_specs = P("wide", "blk", None, None, None)
    return jax.shard_map(body, mesh=mesh, in_specs=in_specs, out_specs=out_specs, check_vma=False)
```

time: 107 us -> 103 us (0.963)
  Pallas kernels: 103 us -> 99.6 us
    pallas_call x1, Pallas kernels: 103 us -> 99.6 us  [ring(): pl.pallas_call(functools.partial(kernel, depth, scale), out_shape=pltpu.V...]
where the time goes in v2:
time: 103 us
  Pallas kernels  99.6 us (97%)
  local copies, waits for them, and re-layouts  3.4 us (3%)
    pallas_call x1, Pallas kernels, ring(): pl.pallas_call(functools.partial(kernel, depth, scale), out_shape=pltpu.V...  99.6 us
    unnamed x1, local copies, waits for them, and re-layouts  3.4 us

profile of v2, /device:TPU:0, one launch (start us, length us, event | category | flops | bytes accessed | tf_op | source)
XLA Modules:
  0.0 103.0 jit_solution(6040711067420156113)
XLA Ops:
  0.0 99.6 %shard_map.46 = f32[2,2,32,128,128]{4,3,2,1,0:T(8,128)S(1)} custom-call(bf16[2,2,128,512]{3,2,1,0:T(8,128)(2,1)} %bitcast.9, bf16[2,2,128,512]{3,2,1,0:T(8,128)(2,1)} %bitcast.10, f32[2,2,32,128,128]{4,3,2,1,0:T(8,128)} %bitcast.8, s32[4,32]{1,0:T(4,128)} %bitcast.11), custom_call_target="tpu_custom_call" | custom-call | tf_op jit(solution)/shard_map/pallas_call | solution.py:572
  99.6 3.4 %copy.7 = f32[4,1,32,128,128]{4,3,2,1,0:T(8,128)} copy(f32[4,1,32,128,128]{4,3,2,1,0:T(8,128)S(1)} %bitcast.7) | data formatting | bytes 16777216

commit v3 on v2

--- a/solution.py
+++ b/solution.py
@@ -63,7 +63,7 @@
 MESH = pl.DeviceIdType.MESH
 
 END = (
-    (1, 0, 0, 0, 1, 0, 2), (0, 1, 0, 1, 0, 1, 0), (0, 1, 1, 1, 0, 1, 1), (2, 0, 0, 0, 1, 1, 0),
+    (0, 1, 0, 1, 0, 3, 0), (1, 0, 0, 0, 1, 2, 2), (0, 1, 1, 1, 0, 3, 1), (2, 0, 0, 0, 1, 1, 0),
     (2, 0, 1, 0, 1, 1, 1), (1, 1, 0, 0, 0, 1, 2), (3, 0, 0, 0, 1, 1, 0), (2, 1, 0, 0, 0, 1, 0),
     (3, 0, 1, 0, 1, 1, 1), (2, 1, 1, 0, 0, 1, 1), (3, 1, 0, 0, 0, 1, 0), (3, 1, 1, 0, 0, 1, 1),
 )
@@ -75,19 +75,19 @@
 )
 STEPS = len(INNER)
 EARLY = (3, 6)
-LAG = 4
+LAG = 3
 BATCH = 8
-ALONG, OVER, CORE, HAND, SWAP, BESIDE, NEAR, PAIR, DIRECT, VIA, ONWARD = range(11)
+ALONG, OVER, CORE, HAND, SWAP, BESIDE, NEAR, PAIR, DIRECT, VIA, ONWARD, SHARE = range(12)
 
 
 def packed(row):
     place, across, u, along, over, handed, kept = row
-    return place + 4 * across + 8 * u + 16 * along + 64 * over + 128 * handed + 256 * kept
+    return place + 4 * across + 8 * u + 16 * along + 64 * over + 128 * handed + 512 * kept
 
 
 def kernel(
     depth, scale, resid, samples, weights, flags, held,
-    own, cols, beside, near, pair, stage, landed, out, got, passing, recv, beside_cols, own_recv,
+    own, cols, beside, near, pair, stage, landed, out, got, passing, shared, recv, beside_cols, own_recv,
     res_recv, beside_recv, near_recv, pair_recv, got_recv, passing_recv, sends, fill,
 ):
     b = lax.axis_index("blk")
@@ -124,8 +124,8 @@
         u = (code // 8) % 2
         along = (code // 16) % 4
         over = (code // 64) % 2
-        handed = (code // 128) % 2
-        kept = code // 256
+        handed = (code // 128) % 4
+        kept = code // 512
         served = jnp.where(place == 0, inner, 0)
         return at(zz, yy, c), at(zz, yy, 1 - c), u, along, over, handed, kept, across, served
 
@@ -154,7 +154,8 @@
         greet(wide=out_target)
 
     greet(wide=at(outward, y, 1 - c))
-    pl.semaphore_wait(barrier, 5 + inner)
+    greet(wide=at(z, 1 - y, 1 - c))
+    pl.semaphore_wait(barrier, 6 + inner)
 
     def whole(ref, sent_sem, took_sem):
         return pltpu.make_async_remote_copy(
@@ -234,6 +235,17 @@
 
     def pair_arrive(d):
         took(pair.at[:, d], pair_recv.at[d])
+
+    def share():
+        return pltpu.make_async_remote_copy(
+            src_ref=shared.at[0], dst_ref=shared.at[1], send_sem=sends.at[SHARE],
+            recv_sem=got_recv.at[2], device_id={"wide": at(z, 1 - y, jnp.where(y == 0, c, 1 - c))},
+            device_id_type=MESH,
+        )
+
+    def hands(handed, d):
+        alone = jnp.where(handed == 2, 1, jnp.where(handed == 3, y, -1))
+        return jnp.logical_or(handed == 1, alone == d)
 
     def outward_core(d):
         return at(outward, y, jnp.where(d == 0, c, 1 - c))
@@ -332,7 +344,7 @@
         def _():
             via(d, p, u).start()
 
-        @pl.when(jnp.where(across == 0, nb, -1) == p)
+        @pl.when(jnp.where(across + d == 0, nb, -1) == p)
         def _():
             for t in range(per - 1):
                 out[0, d, p, u, t] = part(t).T
@@ -371,17 +383,31 @@
         step = decode(n)
         u, handed, across, served = step[2], step[5], step[7], step[8]
 
+        chip = step[0] // 2
+
         @pl.when(handed == 1)
         def _():
-            chip = step[0] // 2
             took(landed.at[pl.ds(2 * chip, 2), u], res_recv.at[chip, u])
-            for d in range(2):
-                panel = step[d]
+
+        @pl.when(handed > 1)
+        def _():
+            took(landed.at[0, u], res_recv.at[chip, u])
+
+        for d in range(2):
+            panel = step[d]
+
+            @pl.when(hands(handed, d))
+            def _():
                 finish(1, panel, u, lambda t: landed[panel, u, t])
 
                 @pl.when(served == 1)
                 def _():
                     emit(across, d, 1, u, lambda t: landed[panel, u, t])
+
+                @pl.when(jnp.where(handed == 3, nb, 0) == 1)
+                def _():
+                    for t in range(per):
+                        shared[0, t, u] = landed[panel, u, t].T
 
     def settle(n, carry):
         receive(n)
@@ -413,7 +439,7 @@
             def _():
                 arrive_beside(u, panel)
 
-            @pl.when(handed == 1)
+            @pl.when(hands(handed, i))
             def _():
                 total = cut(gram(1, lambda h, a: cols[h, panel, u, a]))
                 for t in range(per):
@@ -429,6 +455,12 @@
                     for v in range(per):
                         emit(across, i, 0, v, cut(total, v))
 
+                @pl.when(jnp.where(handed == 3, nb + jnp.where(i == y, 0, 1), 1) == 0)
+                def _():
+                    for v in range(per):
+                        for t in range(per):
+                            shared[0, t, v] = cut(total, v)(t).T
+
             @pl.when(kept == 2)
             def _():
                 finish(0, panel, u, cut(gram(0, lambda h, a: cols[h, panel, u, a])))
@@ -449,12 +481,21 @@
         def _():
             receive(n - LAG)
 
+        @pl.when(jnp.where(inner == 0, n, -1) == BATCH)
+        def _():
+            share().start()
+
         @pl.when(inner == 1)
         def _():
-            @pl.when(n == STEPS - 5)
+            @pl.when(n == STEPS - 9)
             def _():
                 for h in (b, nb):
                     start(near_own(h, 0))
+
+            @pl.when(n == STEPS - 7)
+            def _():
+                for h in (b, nb):
+                    start(near_own(h, 1))
 
             @pl.when(n == STEPS - 4)
             def _():
@@ -462,13 +503,12 @@
                     for d in range(2):
                         for p in range(2):
                             direct(d, p, u, per - 1).start()
-                        for t in range(per - 1):
-                            direct(d, nb, u, t).start()
+                    for t in range(per - 1):
+                        direct(0, nb, u, t).start()
 
             @pl.when(n == STEPS - 2)
             def _():
                 for h in (b, nb):
-                    start(near_own(h, 1))
                     start(pair_own(h))
                 relay(0)
 
@@ -517,7 +557,7 @@
 
         lax.fori_loop(0, 2, adjacent, 0)
 
-        sent(got.at[:3, :, :, 0], DIRECT)
+        sent(held.at[:, 0, :5], DIRECT)
         sent(passing, VIA)
         sent(passing, ONWARD)
         sent(near, NEAR)
@@ -534,8 +574,11 @@
             finish(jnp.where(p == 0, b, nb), panel, t, lambda u: got[k, p, u, t])
 
         def closer(k, carry):
-            for t in range(per - 1):
-                accept(k, t, nb)
+            @pl.when(k == 0)
+            def _():
+                for t in range(per - 1):
+                    accept(k, t, nb)
+
             for p in range(2):
                 accept(k, per - 1, p)
             return carry
@@ -545,18 +588,29 @@
             return carry
 
         lax.fori_loop(count - LAG, count - 2, settle, 0)
-        took(got.at[:3, :, :, 0], got_recv.at[0])
+        took(held.at[:, 0, :5], got_recv.at[0])
         lax.fori_loop(0, 2, closer, 0)
         took(got.at[2:, :, :, per - 1], got_recv.at[1])
         lax.fori_loop(0, 4, farther, 0)
         sent(cols.at[0, :4], ALONG)
         sent(cols.at[0, :7], OVER)
         sent(cols.at[:, :7], CORE)
+        took(shared.at[1], got_recv.at[2])
+        for t in range(per):
+            finish(1, at(z, 1 - y, jnp.where(y == 1, c, 1 - c)), t, lambda u: shared[1, t, u])
+        sent(shared.at[0], SHARE)
 
     sent(own.at[b], SWAP)
     sent(beside, BESIDE)
     lax.fori_loop(count - 2, count, settle, 0)
-    sent(stage.at[:11], HAND)
+
+    @pl.when(inner == 0)
+    def _():
+        sent(held.at[:, 0, :21], HAND)
+
+    @pl.when(inner == 1)
+    def _():
+        sent(held.at[:, 0, :22], HAND)
 
 
 def ring(resid, samples, precision, active):
@@ -585,6 +639,7 @@
             pltpu.VMEM((2, 2, 2, per, per, tile, tile), f32),
             pltpu.VMEM((4, 2, per, per, tile, tile), f32),
             pltpu.VMEM((2, 2, per, tile, tile), f32),
+            pltpu.VMEM((2, per, per, tile, tile), f32),
             dma((2, panels // 2, per)),
             dma((panels // 2, per)),
             dma((3,)),
@@ -592,9 +647,9 @@
             dma((1,)),
             dma((3,)),
             dma((2,)),
-            dma((2,)),
             dma((3,)),
-            dma((11,)),
+            dma((3,)),
+            dma((12,)),
             dma((2,)),
         ],
         compiler_params=pltpu.CompilerParams(

time: 103 us -> 97.7 us (0.949)
  Pallas kernels: 99.6 us -> 94.1 us
    pallas_call x1, Pallas kernels: 99.6 us -> 94.1 us  [ring(): pl.pallas_call(functools.partial(kernel, depth, scale), out_shape=pltpu.V...]
where the time goes in v3:
time: 97.7 us; the launch traced here: 97.5 us
  Pallas kernels  94.1 us (96%)
  local copies, waits for them, and re-layouts  3.4 us (3%)
    pallas_call x1, Pallas kernels, ring(): pl.pallas_call(functools.partial(kernel, depth, scale), out_shape=pltpu.V...  94.1 us
    unnamed x1, local copies, waits for them, and re-layouts  3.4 us

profile of v3, /device:TPU:0, one launch (start us, length us, event | category | flops | bytes accessed | tf_op | source)
XLA Modules:
  0.0 97.5 jit_solution(7382414646456537735)
XLA Ops:
  0.0 94.1 %shard_map.46 = f32[2,2,32,128,128]{4,3,2,1,0:T(8,128)S(1)} custom-call(bf16[2,2,128,512]{3,2,1,0:T(8,128)(2,1)} %bitcast.9, bf16[2,2,128,512]{3,2,1,0:T(8,128)(2,1)} %bitcast.10, f32[2,2,32,128,128]{4,3,2,1,0:T(8,128)} %bitcast.8, s32[4,32]{1,0:T(4,128)} %bitcast.11), custom_call_target="tpu_custom_call" | custom-call | tf_op jit(solution)/shard_map/pallas_call | solution.py:626
  94.1 3.4 %copy.7 = f32[4,1,32,128,128]{4,3,2,1,0:T(8,128)} copy(f32[4,1,32,128,128]{4,3,2,1,0:T(8,128)S(1)} %bitcast.7) | data formatting | bytes 16777216

commit v4 on v3

--- a/solution.py
+++ b/solution.py
@@ -65,11 +65,11 @@
 END = (
     (0, 1, 0, 1, 0, 3, 0), (1, 0, 0, 0, 1, 2, 2), (0, 1, 1, 1, 0, 3, 1), (2, 0, 0, 0, 1, 1, 0),
     (2, 0, 1, 0, 1, 1, 1), (1, 1, 0, 0, 0, 1, 2), (3, 0, 0, 0, 1, 1, 0), (2, 1, 0, 0, 0, 1, 0),
-    (3, 0, 1, 0, 1, 1, 1), (2, 1, 1, 0, 0, 1, 1), (3, 1, 0, 0, 0, 1, 0), (3, 1, 1, 0, 0, 1, 1),
+    (3, 0, 1, 0, 2, 1, 1), (2, 1, 1, 0, 0, 1, 1), (3, 1, 0, 0, 0, 1, 0), (3, 1, 1, 3, 0, 1, 1),
 )
 INNER = (
     (2, 0, 0, 2, 1, 1, 0), (0, 0, 0, 1, 0, 1, 0), (1, 1, 0, 0, 0, 0, 0), (2, 0, 1, 2, 1, 0, 1),
-    (0, 0, 1, 1, 0, 1, 1), (1, 1, 1, 0, 0, 0, 1), (3, 0, 0, 2, 0, 1, 0), (0, 1, 0, 1, 0, 1, 0),
+    (0, 0, 1, 1, 0, 0, 1), (1, 1, 1, 0, 0, 0, 1), (3, 0, 0, 2, 0, 1, 0), (0, 1, 0, 1, 0, 1, 0),
     (2, 1, 0, 0, 0, 1, 0), (3, 0, 1, 2, 0, 1, 1), (0, 1, 1, 1, 0, 1, 1), (2, 1, 1, 0, 0, 1, 1),
     (3, 1, 0, 0, 0, 1, 0), (3, 1, 1, 0, 0, 1, 1),
 )
@@ -77,18 +77,18 @@
 EARLY = (3, 6)
 LAG = 3
 BATCH = 8
-ALONG, OVER, CORE, HAND, SWAP, BESIDE, NEAR, PAIR, DIRECT, VIA, ONWARD, SHARE = range(12)
+ALONG, OVER, CORE, HAND, SWAP, BESIDE, NEAR, PAIR, DIRECT, VIA, ONWARD, SHARE, CROSS = range(13)
 
 
 def packed(row):
     place, across, u, along, over, handed, kept = row
-    return place + 4 * across + 8 * u + 16 * along + 64 * over + 128 * handed + 512 * kept
+    return place + 4 * across + 8 * u + 16 * along + 64 * over + 256 * handed + 1024 * kept
 
 
 def kernel(
     depth, scale, resid, samples, weights, flags, held,
-    own, cols, beside, near, pair, stage, landed, out, got, passing, shared, recv, beside_cols, own_recv,
-    res_recv, beside_recv, near_recv, pair_recv, got_recv, passing_recv, sends, fill,
+    own, cols, beside, near, pair, stage, landed, out, got, passing, shared, crossed, recv, beside_cols, own_recv,
+    res_recv, halves, beside_recv, near_recv, pair_recv, got_recv, passing_recv, sends, crossed_recv, fill,
 ):
     b = lax.axis_index("blk")
     w = lax.axis_index("wide")
@@ -123,9 +123,9 @@
         yy = jnp.where(across == 1, 1 - y, y)
         u = (code // 8) % 2
         along = (code // 16) % 4
-        over = (code // 64) % 2
-        handed = (code // 128) % 4
-        kept = code // 512
+        over = (code // 64) % 4
+        handed = (code // 256) % 4
+        kept = code // 1024
         served = jnp.where(place == 0, inner, 0)
         return at(zz, yy, c), at(zz, yy, 1 - c), u, along, over, handed, kept, across, served
 
@@ -195,7 +195,7 @@
         src = cols.at[h, panel, u]
         target = jnp.where(along == 1, in_target, out_target)
         return (
-            (along > 0, push(h, u, src, panel, ALONG, target)),
+            (along % 3 > 0, push(h, u, src, panel, ALONG, target)),
             (over == 1, push(h, u, src, panel, OVER, y_target)),
             (None, push(h, u, src, panel, CORE, c_target)),
         )
@@ -246,6 +246,12 @@
     def hands(handed, d):
         alone = jnp.where(handed == 2, 1, jnp.where(handed == 3, y, -1))
         return jnp.logical_or(handed == 1, alone == d)
+
+    def cross(h, d, src, target):
+        return pltpu.make_async_remote_copy(
+            src_ref=src, dst_ref=crossed.at[h, d], send_sem=sends.at[CROSS],
+            recv_sem=crossed_recv.at[d], device_id={"wide": target}, device_id_type=MESH,
+        )
 
     def outward_core(d):
         return at(outward, y, jnp.where(d == 0, c, 1 - c))
@@ -353,10 +359,62 @@
         arrive(h, step[2], step[0])
         start(step_pushes(h, step))
 
+    def piece(ref, h, panel, u, j):
+        return ref.at[h, panel, u, :, pl.ds(j * (tile // 2), tile // 2)]
+
+    def half_push(h, panel, u, j, lane, target):
+        sem = halves.at[2 + j] if lane == CORE else halves.at[j]
+        return pltpu.make_async_remote_copy(
+            src_ref=piece(cols, h, panel, u, j), dst_ref=piece(cols, h, panel, u, j),
+            send_sem=sends.at[lane], recv_sem=sem, device_id={"wide": target},
+            device_id_type=MESH,
+        )
+
+    def half_hand(panel, u, j):
+        rows = pl.ds(j * (tile // 2), tile // 2)
+        return pltpu.make_async_remote_copy(
+            src_ref=stage.at[panel, u, :, rows], dst_ref=landed.at[panel, u, :, rows],
+            send_sem=sends.at[HAND], recv_sem=res_recv.at[panel // 2, u],
+            device_id={"blk": nb}, device_id_type=MESH,
+        )
+
+    def by_halves(step):
+        u = step[2]
+        for j in range(2):
+            rows = pl.ds(j * (tile // 2), tile // 2)
+            for d in range(2):
+                panel = step[d]
+                took(cols.at[:, panel, u, :, rows], halves.at[2 * d + j])
+                if d == 0:
+                    for h in (b, nb):
+                        half_push(h, panel, u, j, CORE, c_target).start()
+                total = None
+                for h in range(2):
+                    for a in range(2):
+                        part = lax.dot_general(
+                            cols[h, panel, u, a, rows],
+                            own[h, 1, :, 1 - a].reshape(per * tile, -1),
+                            (((1,), (1,)), ((), ())), preferred_element_type=jnp.float32,
+                        )
+                        total = part if total is None else total + part
+                total = total * scale
+                for t in range(per):
+                    stage[panel, u, t, rows] = total[:, t * tile:(t + 1) * tile]
+                half_hand(panel, u, j).start()
+
     def forward(n):
         step = decode(n)
-        for h in (b, nb):
-            pass_on(h, step)
+
+        @pl.when(step[3] < 3)
+        def _():
+            for h in (b, nb):
+                pass_on(h, step)
+
+        @pl.when(step[4] == 2)
+        def _():
+            for j in range(2):
+                for h in (b, nb):
+                    half_push(h, step[0], step[2], j, OVER, y_target).start()
 
     pltpu.make_async_copy(own.at[b], own.at[b], fill.at[0]).wait()
     for i in range(2):
@@ -374,8 +432,17 @@
         forward(n)
         return carry
 
+    def reached(n):
+        mid = jnp.where(n < 12, 3 * (jnp.maximum(n, 0) // 3) + 3, n + 1)
+        return jnp.maximum(ahead, jnp.where(inner == 1, mid, n + 1))
+
     lax.fori_loop(0, ahead, early, 0)
     took(own.at[nb, nb], own_recv.at[2])
+
+    @pl.when(inner == 0)
+    def _():
+        for h in (b, nb):
+            cross(h, 0, own.at[h, nb, per - 1], in_target).start()
     start(beside_push(nb))
     load_weights.wait()
 
@@ -396,7 +463,11 @@
         for d in range(2):
             panel = step[d]
 
-            @pl.when(hands(handed, d))
+            @pl.when(step[3] == 3)
+            def _():
+                finish(1, panel, u, lambda t: landed[panel, u, t].T)
+
+            @pl.when(hands(jnp.where(step[3] == 3, 0, handed), d))
             def _():
                 finish(1, panel, u, lambda t: landed[panel, u, t])
 
@@ -424,22 +495,23 @@
         finish_all(1, c_target, gram(1, lambda h, a: beside[h, :, a]))
 
     def compute(n, carry):
-        f = n + 2 * inner
-
-        @pl.when(jnp.logical_and(f >= ahead, f < count))
-        def _():
-            forward(f)
-
-        first, second, u, _, _, handed, kept, across, served = decode(n)
+        lax.fori_loop(reached(n - 1), reached(n), early, 0)
+
+        step = decode(n)
+        first, second, u, along, _, handed, kept, across, served = step
+
+        @pl.when(along == 3)
+        def _():
+            by_halves(step)
 
         def both(i, carry):
             panel = jnp.where(i == 0, first, second)
 
-            @pl.when(i == 1)
+            @pl.when(jnp.where(along == 3, 0, i) == 1)
             def _():
                 arrive_beside(u, panel)
 
-            @pl.when(hands(handed, i))
+            @pl.when(hands(jnp.where(along == 3, 0, handed), i))
             def _():
                 total = cut(gram(1, lambda h, a: cols[h, panel, u, a]))
                 for t in range(per):
@@ -494,22 +566,50 @@
 
             @pl.when(n == STEPS - 7)
             def _():
-                for h in (b, nb):
-                    start(near_own(h, 1))
+                start(near_own(b, 1))
+
+            @pl.when(n == BATCH + 1)
+            def _():
+                for d in range(2):
+                    direct(d, 0, 0, per - 1).start()
+                    direct(d, 1, 0, per - 1).start()
+                    direct(d, 0, 1, per - 1).start()
+                direct(0, nb, 0, 0).start()
+
+                @pl.when(nb == 0)
+                def _():
+                    direct(0, 0, 1, 0).start()
 
             @pl.when(n == STEPS - 4)
             def _():
-                for u in range(per):
-                    for d in range(2):
-                        for p in range(2):
-                            direct(d, p, u, per - 1).start()
-                    for t in range(per - 1):
-                        direct(0, nb, u, t).start()
-
-            @pl.when(n == STEPS - 2)
-            def _():
+                start(near_own(nb, 1))
                 for h in (b, nb):
                     start(pair_own(h))
+
+            @pl.when(n == STEPS - 3)
+            def _():
+                took(crossed.at[:, 0], crossed_recv.at[0])
+                for h in (b, nb):
+                    cross(h, 1, crossed.at[h, 0], c_target).start()
+
+            @pl.when(n == STEPS - 2)
+            def _():
+                took(crossed.at[:, 1], crossed_recv.at[1])
+
+            @pl.when(jnp.logical_or(n == STEPS - 3, n == STEPS - 2))
+            def _():
+                d = n - (STEPS - 3)
+                total = cut(gram(1, lambda h, a: crossed[h, d, a]))
+                finish(1, at(outward, y, jnp.where(d == 0, c, 1 - c)), per - 1, total)
+                emit(0, d, 1, per - 1, total)
+                direct(d, 1, per - 1, per - 1).start()
+
+                @pl.when(jnp.where(d == 0, nb, 0) == 1)
+                def _():
+                    direct(0, 1, per - 1, 0).start()
+
+            @pl.when(n == STEPS - 2)
+            def _():
                 relay(0)
 
             @pl.when(n == STEPS - 1)
@@ -530,11 +630,11 @@
 
     @pl.when(inner == 1)
     def _():
-        receive(count - LAG)
         near_arrive(0)
         for h in (b, nb):
             start(near_relay(h, 0))
         relay(2)
+        receive(count - LAG)
         lax.fori_loop(count - LAG + 1, count - 2, settle, 0)
         near_arrive(1)
         for h in (b, nb):
@@ -562,6 +662,7 @@
         sent(passing, ONWARD)
         sent(near, NEAR)
         sent(pair, PAIR)
+        sent(crossed.at[:, 0], CROSS)
         sent(cols.at[0, :11], ALONG)
         sent(cols.at[0, :4], OVER)
         sent(cols.at[:, :8], CORE)
@@ -599,6 +700,7 @@
         for t in range(per):
             finish(1, at(z, 1 - y, jnp.where(y == 1, c, 1 - c)), t, lambda u: shared[1, t, u])
         sent(shared.at[0], SHARE)
+        sent(crossed.at[:, 0], CROSS)
 
     sent(own.at[b], SWAP)
     sent(beside, BESIDE)
@@ -610,7 +712,7 @@
 
     @pl.when(inner == 1)
     def _():
-        sent(held.at[:, 0, :22], HAND)
+        sent(held.at[:, 0, :20], HAND)
 
 
 def ring(resid, samples, precision, active):
@@ -640,16 +742,19 @@
             pltpu.VMEM((4, 2, per, per, tile, tile), f32),
             pltpu.VMEM((2, 2, per, tile, tile), f32),
             pltpu.VMEM((2, per, per, tile, tile), f32),
+            pltpu.VMEM((2, 2, 2, tile, half), bf16),
             dma((2, panels // 2, per)),
             dma((panels // 2, per)),
             dma((3,)),
             dma((panels // 2, per)),
+            dma((4,)),
             dma((1,)),
             dma((3,)),
             dma((2,)),
             dma((3,)),
             dma((3,)),
-            dma((12,)),
+            dma((13,)),
+            dma((2,)),
             dma((2,)),
         ],
         compiler_params=pltpu.CompilerParams(

time: 97.7 us -> 95.9 us (0.982)
  Pallas kernels: 94.1 us -> 92.3 us
    pallas_call x1, Pallas kernels: 94.1 us -> 92.3 us  [ring(): pl.pallas_call(functools.partial(kernel, depth, scale), out_shape=pltpu.V...]
where the time goes in v4:
time: 95.9 us; the launch traced here: 95.7 us
  Pallas kernels  92.3 us (96%)
  local copies, waits for them, and re-layouts  3.4 us (4%)
    pallas_call x1, Pallas kernels, ring(): pl.pallas_call(functools.partial(kernel, depth, scale), out_shape=pltpu.V...  92.3 us
    unnamed x1, local copies, waits for them, and re-layouts  3.4 us

profile of v4, /device:TPU:0, one launch (start us, length us, event | category | flops | bytes accessed | tf_op | source)
XLA Modules:
  0.0 95.7 jit_solution(7297015493378379759)
XLA Ops:
  0.0 92.3 %shard_map.46 = f32[2,2,32,128,128]{4,3,2,1,0:T(8,128)S(1)} custom-call(bf16[2,2,128,512]{3,2,1,0:T(8,128)(2,1)} %bitcast.9, bf16[2,2,128,512]{3,2,1,0:T(8,128)(2,1)} %bitcast.10, f32[2,2,32,128,128]{4,3,2,1,0:T(8,128)} %bitcast.8, s32[4,32]{1,0:T(4,128)} %bitcast.11), custom_call_target="tpu_custom_call" | custom-call | tf_op jit(solution)/shard_map/pallas_call | solution.py:728
  92.3 3.4 %copy.7 = f32[4,1,32,128,128]{4,3,2,1,0:T(8,128)} copy(f32[4,1,32,128,128]{4,3,2,1,0:T(8,128)S(1)} %bitcast.7) | data formatting | bytes 16777216

commit v5 on v4

--- a/solution.py
+++ b/solution.py
@@ -63,9 +63,9 @@
 MESH = pl.DeviceIdType.MESH
 
 END = (
-    (0, 1, 0, 1, 0, 3, 0), (1, 0, 0, 0, 1, 2, 2), (0, 1, 1, 1, 0, 3, 1), (2, 0, 0, 0, 1, 1, 0),
-    (2, 0, 1, 0, 1, 1, 1), (1, 1, 0, 0, 0, 1, 2), (3, 0, 0, 0, 1, 1, 0), (2, 1, 0, 0, 0, 1, 0),
-    (3, 0, 1, 0, 2, 1, 1), (2, 1, 1, 0, 0, 1, 1), (3, 1, 0, 0, 0, 1, 0), (3, 1, 1, 3, 0, 1, 1),
+    (0, 1, 0, 1, 0, 3, 0), (1, 0, 0, 0, 1, 2, 2), (0, 1, 1, 1, 0, 4, 1), (2, 0, 0, 0, 1, 1, 0),
+    (1, 1, 0, 0, 0, 1, 2), (2, 0, 1, 0, 1, 1, 1), (2, 1, 0, 0, 0, 1, 0), (3, 0, 0, 0, 1, 1, 0),
+    (2, 1, 1, 0, 0, 1, 1), (3, 0, 1, 0, 2, 1, 1), (3, 1, 0, 0, 0, 1, 0), (3, 1, 1, 3, 0, 1, 1),
 )
 INNER = (
     (2, 0, 0, 2, 1, 1, 0), (0, 0, 0, 1, 0, 1, 0), (1, 1, 0, 0, 0, 0, 0), (2, 0, 1, 2, 1, 0, 1),
@@ -77,12 +77,13 @@
 EARLY = (3, 6)
 LAG = 3
 BATCH = 8
+PARTS = 4
 ALONG, OVER, CORE, HAND, SWAP, BESIDE, NEAR, PAIR, DIRECT, VIA, ONWARD, SHARE, CROSS = range(13)
 
 
 def packed(row):
     place, across, u, along, over, handed, kept = row
-    return place + 4 * across + 8 * u + 16 * along + 64 * over + 256 * handed + 1024 * kept
+    return place + 4 * across + 8 * u + 16 * along + 64 * over + 256 * handed + 2048 * kept
 
 
 def kernel(
@@ -124,9 +125,9 @@
         u = (code // 8) % 2
         along = (code // 16) % 4
         over = (code // 64) % 4
-        handed = (code // 256) % 4
-        kept = code // 1024
-        served = jnp.where(place == 0, inner, 0)
+        handed = (code // 256) % 8
+        kept = code // 2048
+        served = jnp.where(place == 0, 1 + inner, 0)
         return at(zz, yy, c), at(zz, yy, 1 - c), u, along, over, handed, kept, across, served
 
     loads = []
@@ -244,8 +245,11 @@
         )
 
     def hands(handed, d):
-        alone = jnp.where(handed == 2, 1, jnp.where(handed == 3, y, -1))
+        alone = jnp.where(handed == 2, 1, jnp.where(handed >= 3, y, -1))
         return jnp.logical_or(handed == 1, alone == d)
+
+    def lower(handed, d):
+        return jnp.where(handed == 4, jnp.where(d == y, 0, 1), 0) == 1
 
     def cross(h, d, src, target):
         return pltpu.make_async_remote_copy(
@@ -288,7 +292,7 @@
         p = (nb, b)[i] if h is b else (b, nb)[i]
         return pltpu.make_async_remote_copy(
             src_ref=own.at[h, p, t], dst_ref=own.at[h, p, t], send_sem=sends.at[SWAP],
-            recv_sem=own_recv.at[t if i == 0 else 2], device_id={"blk": nb}, device_id_type=MESH,
+            recv_sem=own_recv.at[2 * i + t], device_id={"blk": nb}, device_id_type=MESH,
         )
 
     def hand(panel, u):
@@ -310,15 +314,15 @@
                 total = part if total is None else total + part
         return total * scale
 
-    def finish(p, panel, u, part, diagonal=False):
-        for t in range(per):
+    def finish(p, panel, u, part, diagonal=False, rows=None):
+        for t in range(per) if rows is None else rows:
             slot = panel * per + u
             weight = held[t, p, slot]
             half = part(t) + RIDGE * weight
             if diagonal and t == u:
-                rows = lax.broadcasted_iota(jnp.int32, (tile, tile), 0)
+                lines = lax.broadcasted_iota(jnp.int32, (tile, tile), 0)
                 columns = lax.broadcasted_iota(jnp.int32, (tile, tile), 1)
-                on_diag = rows == columns + b * (2 * tile)
+                on_diag = lines == columns + b * (2 * tile)
                 inverse = jnp.where(on_diag, 1.0 / jnp.where(on_diag, weight, 1.0), 0.0)
                 stepped = weight - STEP * (half - inverse)
             else:
@@ -360,10 +364,10 @@
         start(step_pushes(h, step))
 
     def piece(ref, h, panel, u, j):
-        return ref.at[h, panel, u, :, pl.ds(j * (tile // 2), tile // 2)]
+        return ref.at[h, panel, u, :, pl.ds(j * (tile // PARTS), tile // PARTS)]
 
     def half_push(h, panel, u, j, lane, target):
-        sem = halves.at[2 + j] if lane == CORE else halves.at[j]
+        sem = halves.at[PARTS + j] if lane == CORE else halves.at[j]
         return pltpu.make_async_remote_copy(
             src_ref=piece(cols, h, panel, u, j), dst_ref=piece(cols, h, panel, u, j),
             send_sem=sends.at[lane], recv_sem=sem, device_id={"wide": target},
@@ -371,7 +375,7 @@
         )
 
     def half_hand(panel, u, j):
-        rows = pl.ds(j * (tile // 2), tile // 2)
+        rows = pl.ds(j * (tile // PARTS), tile // PARTS)
         return pltpu.make_async_remote_copy(
             src_ref=stage.at[panel, u, :, rows], dst_ref=landed.at[panel, u, :, rows],
             send_sem=sends.at[HAND], recv_sem=res_recv.at[panel // 2, u],
@@ -380,11 +384,11 @@
 
     def by_halves(step):
         u = step[2]
-        for j in range(2):
-            rows = pl.ds(j * (tile // 2), tile // 2)
+        for j in range(PARTS):
+            rows = pl.ds(j * (tile // PARTS), tile // PARTS)
             for d in range(2):
                 panel = step[d]
-                took(cols.at[:, panel, u, :, rows], halves.at[2 * d + j])
+                took(cols.at[:, panel, u, :, rows], halves.at[PARTS * d + j])
                 if d == 0:
                     for h in (b, nb):
                         half_push(h, panel, u, j, CORE, c_target).start()
@@ -412,7 +416,7 @@
 
         @pl.when(step[4] == 2)
         def _():
-            for j in range(2):
+            for j in range(PARTS):
                 for h in (b, nb):
                     half_push(h, step[0], step[2], j, OVER, y_target).start()
 
@@ -436,8 +440,38 @@
         mid = jnp.where(n < 12, 3 * (jnp.maximum(n, 0) // 3) + 3, n + 1)
         return jnp.maximum(ahead, jnp.where(inner == 1, mid, n + 1))
 
-    lax.fori_loop(0, ahead, early, 0)
-    took(own.at[nb, nb], own_recv.at[2])
+    def row_hand(panel, u, t, lane=HAND):
+        total = None
+        for h in range(2):
+            for a in range(2):
+                part = lax.dot_general(
+                    own[h, 1, t, a], cols[h, panel, u, 1 - a], (((1,), (1,)), ((), ())),
+                    preferred_element_type=jnp.float32,
+                )
+                total = part if total is None else total + part
+        stage[panel, u, t] = total * scale
+        pltpu.make_async_remote_copy(
+            src_ref=stage.at[panel, u, t], dst_ref=landed.at[panel, u, t],
+            send_sem=sends.at[lane], recv_sem=res_recv.at[panel // 2, u],
+            device_id={"blk": nb}, device_id_type=MESH,
+        ).start()
+
+    lax.fori_loop(0, 2, early, 0)
+    took(own.at[nb, nb, 0], own_recv.at[2])
+
+    @pl.when(inner == 0)
+    def _():
+        def first_row(n, carry):
+            first, second, u = decode(n)[:3]
+            arrive_beside(u, second)
+            row_hand(jnp.where(jnp.where(n == 0, y, 1) == 0, first, second), u, 0)
+            return carry
+
+        lax.fori_loop(0, 2, first_row, 0)
+
+    lax.fori_loop(2, ahead, early, 0)
+    for t in range(1, per):
+        took(own.at[nb, nb, t], own_recv.at[2 + t])
 
     @pl.when(inner == 0)
     def _():
@@ -456,13 +490,21 @@
         def _():
             took(landed.at[pl.ds(2 * chip, 2), u], res_recv.at[chip, u])
 
-        @pl.when(handed > 1)
+        @pl.when(jnp.where(handed == 4, 0, handed) > 1)
         def _():
             took(landed.at[0, u], res_recv.at[chip, u])
+
+        @pl.when(handed == 4)
+        def _():
+            took(held.at[0, 0, :3], res_recv.at[chip, u])
 
         for d in range(2):
             panel = step[d]
 
+            @pl.when(lower(handed, d))
+            def _():
+                finish(1, panel, u, lambda t: landed[panel, u, t], rows=(per - 1,))
+
             @pl.when(step[3] == 3)
             def _():
                 finish(1, panel, u, lambda t: landed[panel, u, t].T)
@@ -471,14 +513,17 @@
             def _():
                 finish(1, panel, u, lambda t: landed[panel, u, t])
 
-                @pl.when(served == 1)
+                @pl.when(served == 2)
                 def _():
                     emit(across, d, 1, u, lambda t: landed[panel, u, t])
 
-                @pl.when(jnp.where(handed == 3, nb, 0) == 1)
+                @pl.when(jnp.where(served == 1, nb + jnp.where(d == y, 1, 0), 0) == 2)
                 def _():
-                    for t in range(per):
-                        shared[0, t, u] = landed[panel, u, t].T
+                    shared[0, u] = landed[panel, u, 0].T
+
+                    @pl.when(u == 0)
+                    def _():
+                        shared[0, 2] = landed[panel, u, 1].T
 
     def settle(n, carry):
         receive(n)
@@ -500,6 +545,8 @@
         step = decode(n)
         first, second, u, along, _, handed, kept, across, served = step
 
+        begun = jnp.logical_and(n < 2, inner == 0)
+
         @pl.when(along == 3)
         def _():
             by_halves(step)
@@ -507,31 +554,40 @@
         def both(i, carry):
             panel = jnp.where(i == 0, first, second)
 
-            @pl.when(jnp.where(along == 3, 0, i) == 1)
+            @pl.when(jnp.where(along == 3, 0, jnp.where(begun, 0, i)) == 1)
             def _():
                 arrive_beside(u, panel)
 
-            @pl.when(hands(jnp.where(along == 3, 0, handed), i))
+            @pl.when(hands(jnp.where(begun, handed, 0), i))
+            def _():
+                for t in range(1, per):
+                    row_hand(panel, u, t)
+
+            @pl.when(hands(jnp.where(along == 3, 0, jnp.where(begun, 0, handed)), i))
             def _():
                 total = cut(gram(1, lambda h, a: cols[h, panel, u, a]))
                 for t in range(per):
                     stage[panel, u, t] = total(t)
                 hand(panel, u).start()
 
+            @pl.when(lower(handed, i))
+            def _():
+                row_hand(panel, u, per - 1, SHARE)
+
             @pl.when(kept == 1)
             def _():
                 total = keep(panel)
 
-                @pl.when(served == 1)
+                @pl.when(served == 2)
                 def _():
                     for v in range(per):
                         emit(across, i, 0, v, cut(total, v))
 
-                @pl.when(jnp.where(handed == 3, nb + jnp.where(i == y, 0, 1), 1) == 0)
+                @pl.when(jnp.where(served == 1, nb + jnp.where(i == y, 0, 1), 1) == 0)
                 def _():
                     for v in range(per):
-                        for t in range(per):
-                            shared[0, t, v] = cut(total, v)(t).T
+                        shared[0, v] = cut(total, v)(0).T
+                    shared[0, 2] = cut(total, 0)(1).T
 
             @pl.when(kept == 2)
             def _():
@@ -553,7 +609,7 @@
         def _():
             receive(n - LAG)
 
-        @pl.when(jnp.where(inner == 0, n, -1) == BATCH)
+        @pl.when(jnp.where(inner == 0, n, -1) == BATCH + 1)
         def _():
             share().start()
 
@@ -697,9 +753,10 @@
         sent(cols.at[0, :7], OVER)
         sent(cols.at[:, :7], CORE)
         took(shared.at[1], got_recv.at[2])
-        for t in range(per):
-            finish(1, at(z, 1 - y, jnp.where(y == 1, c, 1 - c)), t, lambda u: shared[1, t, u])
-        sent(shared.at[0], SHARE)
+        other = at(z, 1 - y, jnp.where(y == 1, c, 1 - c))
+        finish(1, other, 0, lambda t: shared[1, t])
+        finish(1, other, 1, lambda t: shared[1, 2], rows=(0,))
+        sent(held.at[0, 0, :4], SHARE)
         sent(crossed.at[:, 0], CROSS)
 
     sent(own.at[b], SWAP)
@@ -741,13 +798,13 @@
             pltpu.VMEM((2, 2, 2, per, per, tile, tile), f32),
             pltpu.VMEM((4, 2, per, per, tile, tile), f32),
             pltpu.VMEM((2, 2, per, tile, tile), f32),
-            pltpu.VMEM((2, per, per, tile, tile), f32),
+            pltpu.VMEM((2, per + 1, tile, tile), f32),
             pltpu.VMEM((2, 2, 2, tile, half), bf16),
             dma((2, panels // 2, per)),
             dma((panels // 2, per)),
-            dma((3,)),
+            dma((4,)),
             dma((panels // 2, per)),
-            dma((4,)),
+            dma((2 * PARTS,)),
             dma((1,)),
             dma((3,)),
             dma((2,)),

time: 95.9 us -> 95.3 us (level)
  no operation moved by 1% of the time
where the time goes in v5:
time: 95.3 us; the launch traced here: 95.2 us
  Pallas kernels  91.7 us (96%)
  local copies, waits for them, and re-layouts  3.4 us (4%)
    pallas_call x1, Pallas kernels, ring(): pl.pallas_call(functools.partial(kernel, depth, scale), out_shape=pltpu.V...  91.7 us
    unnamed x1, local copies, waits for them, and re-layouts  3.4 us

profile of v5, /device:TPU:0, one launch (start us, length us, event | category | flops | bytes accessed | tf_op | source)
XLA Modules:
  0.0 95.2 jit_solution(1593010206205439503)
XLA Ops:
  0.0 91.7 %shard_map.46 = f32[2,2,32,128,128]{4,3,2,1,0:T(8,128)S(1)} custom-call(bf16[2,2,128,512]{3,2,1,0:T(8,128)(2,1)} %bitcast.9, bf16[2,2,128,512]{3,2,1,0:T(8,128)(2,1)} %bitcast.10, f32[2,2,32,128,128]{4,3,2,1,0:T(8,128)} %bitcast.8, s32[4,32]{1,0:T(4,128)} %bitcast.11), custom_call_target="tpu_custom_call" | custom-call | tf_op jit(solution)/shard_map/pallas_call | solution.py:785
  91.8 3.4 %copy.7 = f32[4,1,32,128,128]{4,3,2,1,0:T(8,128)} copy(f32[4,1,32,128,128]{4,3,2,1,0:T(8,128)S(1)} %bitcast.7) | data formatting | bytes 16777216

commit v6 on v5

--- a/solution.py
+++ b/solution.py
@@ -63,7 +63,7 @@
 MESH = pl.DeviceIdType.MESH
 
 END = (
-    (0, 1, 0, 1, 0, 3, 0), (1, 0, 0, 0, 1, 2, 2), (0, 1, 1, 1, 0, 4, 1), (2, 0, 0, 0, 1, 1, 0),
+    (0, 1, 0, 1, 0, 3, 0), (1, 0, 0, 0, 1, 2, 2), (0, 1, 1, 1, 0, 3, 1), (2, 0, 0, 0, 1, 1, 0),
     (1, 1, 0, 0, 0, 1, 2), (2, 0, 1, 0, 1, 1, 1), (2, 1, 0, 0, 0, 1, 0), (3, 0, 0, 0, 1, 1, 0),
     (2, 1, 1, 0, 0, 1, 1), (3, 0, 1, 0, 2, 1, 1), (3, 1, 0, 0, 0, 1, 0), (3, 1, 1, 3, 0, 1, 1),
 )
@@ -519,11 +519,8 @@
 
                 @pl.when(jnp.where(served == 1, nb + jnp.where(d == y, 1, 0), 0) == 2)
                 def _():
-                    shared[0, u] = landed[panel, u, 0].T
-
-                    @pl.when(u == 0)
-                    def _():
-                        shared[0, 2] = landed[panel, u, 1].T
+                    for t in range(per):
+                        shared[0, 2 * t + u] = landed[panel, u, t].T
 
     def settle(n, carry):
         receive(n)
@@ -586,8 +583,8 @@
                 @pl.when(jnp.where(served == 1, nb + jnp.where(i == y, 0, 1), 1) == 0)
                 def _():
                     for v in range(per):
-                        shared[0, v] = cut(total, v)(0).T
-                    shared[0, 2] = cut(total, 0)(1).T
+                        for t in range(per):
+                            shared[0, 2 * t + v] = cut(total, v)(t).T
 
             @pl.when(kept == 2)
             def _():
@@ -754,8 +751,8 @@
         sent(cols.at[:, :7], CORE)
         took(shared.at[1], got_recv.at[2])
         other = at(z, 1 - y, jnp.where(y == 1, c, 1 - c))
-        finish(1, other, 0, lambda t: shared[1, t])
-        finish(1, other, 1, lambda t: shared[1, 2], rows=(0,))
+        for u in range(per):
+            finish(1, other, u, lambda t: shared[1, 2 * u + t])
         sent(held.at[0, 0, :4], SHARE)
         sent(crossed.at[:, 0], CROSS)
 
@@ -798,7 +795,7 @@
             pltpu.VMEM((2, 2, 2, per, per, tile, tile), f32),
             pltpu.VMEM((4, 2, per, per, tile, tile), f32),
             pltpu.VMEM((2, 2, per, tile, tile), f32),
-            pltpu.VMEM((2, per + 1, tile, tile), f32),
+            pltpu.VMEM((2, 2 * per, tile, tile), f32),
             pltpu.VMEM((2, 2, 2, tile, half), bf16),
             dma((2, panels // 2, per)),
             dma((panels // 2, per)),

time: 95.3 us -> 95.3 us (level)
  no operation moved by 1% of the time
where the time goes in v6:
time: 95.3 us; the launch traced here: 95.2 us
  Pallas kernels  91.7 us (96%)
  local copies, waits for them, and re-layouts  3.4 us (4%)
    pallas_call x1, Pallas kernels, ring(): pl.pallas_call(functools.partial(kernel, depth, scale), out_shape=pltpu.V...  91.7 us
    unnamed x1, local copies, waits for them, and re-layouts  3.4 us

profile of v6, /device:TPU:0, one launch (start us, length us, event | category | flops | bytes accessed | tf_op | source)
XLA Modules:
  0.0 95.2 jit_solution(12289017296737976860)
XLA Ops:
  0.0 91.7 %shard_map.46 = f32[2,2,32,128,128]{4,3,2,1,0:T(8,128)S(1)} custom-call(bf16[2,2,128,512]{3,2,1,0:T(8,128)(2,1)} %bitcast.9, bf16[2,2,128,512]{3,2,1,0:T(8,128)(2,1)} %bitcast.10, f32[2,2,32,128,128]{4,3,2,1,0:T(8,128)} %bitcast.8, s32[4,32]{1,0:T(4,128)} %bitcast.11), custom_call_target="tpu_custom_call" | custom-call | tf_op jit(solution)/shard_map/pallas_call | solution.py:782
  91.8 3.4 %copy.7 = f32[4,1,32,128,128]{4,3,2,1,0:T(8,128)} copy(f32[4,1,32,128,128]{4,3,2,1,0:T(8,128)S(1)} %bitcast.7) | data formatting | bytes 16777216
